TPU v7x, 128 devices: a whole 4x4x4 slice. The times are simulated.
128 devices in a mesh: grp: 4 (over z), work: 32 (over y, x, core).
Axes of the slice: x: 4, y: 4, z: 4, core: 2. Of those that a mesh axis runs over, the one named last changes fastest.
Arguments:
- embeddings: bfloat16 [131072, 1024], P(('grp', 'work')), may hold values from -250 to 250
- offsets: int32 [257], replicated, may hold values from 0 to 131072, as said below
Outputs:
- best_match: float32 [131072], P(('grp', 'work'))
Inputs may be any that keep to these rules, and one draw needn't show every extreme that they name: offsets[0] is 0 and each later entry exceeds the one before by 512 to 6144 rows, by exactly 6144 at least once, except that the last cluster may be shorter so as to end at 131072; all entries after it equal 131072. Cluster c holds rows offsets[c] up to offsets[c+1] - 1.
All inputs are finite; a program needn't handle non-finite values.
Results may differ from a plain program's by a relative error of at most 0.00048.
Values may be sent and summed in bfloat16 or wider, within the bound.
A program may use at most 64 MiB of HBM per device.

v0:
```python
import math

import jax
import jax.numpy as jnp
from jax import lax
from jax.sharding import PartitionSpec as P

REACH = 6


def shifted(block, axis, distance):
    devices = range(lax.axis_size(axis))
    route = [(i - distance, i) for i in devices if i - distance in devices]
    return lax.ppermute(block, axis, route)


def to_unit(values):
    widened = values.astype(jnp.float32)
    factor = lax.rsqrt(jnp.mean(widened * widened, axis=1, keepdims=True) + 1e-06) / math.sqrt(
        values.shape[1]
    )
    return (widened * factor).astype(jnp.bfloat16)


def cluster_of(offsets, first_row, row_count, all_rows):
    row_index = first_row + jnp.arange(row_count, dtype=jnp.int32)
    counted = jnp.sum((offsets[None, 1:] <= row_index[:, None]).astype(jnp.int32), axis=1)
    return jnp.where((row_index < 0) | (row_index >= all_rows), -1, counted)


def pair_tile(left_rows, right_rows, left_ids, right_ids, same_block):
    scores = lax.dot_general(
        left_rows, right_rows, (((1,), (1,)), ((), ())), preferred_element_type=jnp.float32
    )
    same_cluster = left_ids[:, None] == right_ids[None, :]
    if same_block:
        positions = jnp.arange(left_ids.shape[0], dtype=jnp.int32)
        same_cluster = same_cluster & (positions[:, None] != positions[None, :])
    masked = jnp.where(same_cluster, scores, -1.0)
    return (jnp.max(masked, axis=1), jnp.max(masked, axis=0))


def guarded(left_rows, right_rows, left_ids, right_ids):
    return pair_tile(left_rows, right_rows, left_ids, right_ids, False)


def shards(embeddings, offsets):
    row_count = embeddings.shape[0]
    all_rows = row_count * lax.axis_size(("grp", "work"))
    unit_rows = to_unit(embeddings)
    first_row = lax.axis_index(("grp", "work")) * row_count
    own_ids = cluster_of(offsets, first_row, row_count, all_rows)
    best_score = pair_tile(unit_rows, unit_rows, own_ids, own_ids, True)[0]
    carried = unit_rows

    def advance(distance, loop_state):
        ahead_rows, carried, best_score = loop_state
        ahead_rows = shifted(ahead_rows, ("grp", "work"), -1)
        ahead_ids = cluster_of(offsets, first_row + distance * row_count, row_count, all_rows)
        row_best, column_best = guarded(unit_rows, ahead_rows, own_ids, ahead_ids)
        best_score = jnp.maximum(best_score, row_best)
        carried = shifted(carried, ("grp", "work"), 1)
        behind_ids = cluster_of(offsets, first_row - distance * row_count, row_count, all_rows)
        best_score = jnp.maximum(best_score, guarded(unit_rows, carried, own_ids, behind_ids)[0])
        return (ahead_rows, carried, best_score)

    loop_state = lax.fori_loop(1, REACH + 1, advance, (unit_rows, carried, best_score))
    best_score = loop_state[2]
    return best_score


def solution(mesh):
    return jax.shard_map(
        shards,
        mesh=mesh,
        in_specs=(P(("grp", "work"), None), P()),
        out_specs=P(("grp", "work")),
        check_vma=False,
    )
```

profile of v0, /device:TPU:64, one launch (start us, length us, event | category | flops | bytes accessed | tf_op | source)
XLA Modules:
  0.0 275.8 jit_solution(1734231846435891589)
XLA Ops:
  0.0 0.9 slice.11
  0.9 2.1 fusion
  3.0 0.4 convert_reduce_fusion.2
  3.4 0.4 fusion.1
  3.8 2.6 select_reduce_fusion.2
  6.4 1.3 copy.5
  7.8 1.3 copy.4
  9.1 266.1 %while.17 = (s32[]{:T(128)}, bf16[1024,1024]{1,0:T(8,128)(2,1)}, bf16[1024,1024]{1,0:T(8,128)(2,1)}, f32[1024]{0:T(1024)S(1)}, s32[1024]{0:T(1024)S(1)}, /*index...) while((s32[]{:T(128)}, bf16[1024,1024]{1,0:T(8,128)(2,1)}, ...), condition=%wide.region_8.9_spmd, body=%wide.region_3.8_spmd.sunk | while | flops 4302841856 | bytes 42028292 | solution.py:67
  9.1 1.9 collective-permute-start.1
  11.0 7.9 %collective-permute-start = (bf16[1024,1024]{1,0:T(8,128)(2,1)}, bf16[1024,1024]{1,0:T(8,128)(2,1)}, u32[]{:S(2)}, u32[]{:S(2)}) collective-permute-start(bf16[1024,1024]{1,0:T(8,128)(2,1)} %get-tuple-element.233), channel_id=1, source_target_pairs={{1,0},{2,1},{3,2},{4,3},{5,4},{6,5},{7,6},{8,7},{9,8},{10,9},{11,1... | collective-permute-start | bytes 6291464 | tf_op jit(solution)/shard_map/while/body/eval_jaxpr/ppermute | solution.py:14
  18.9 0.1 slice.13
  19.0 0.6 convert_reduce_fusion.4
  19.6 21.2 %collective-permute-done.1 = bf16[1024,1024]{1,0:T(8,128)(2,1)S(1)} collective-permute-done((bf16[1024,1024]{1,0:T(8,128)(2,1)}, bf16[1024,1024]{1,0:T(8,128)(2,1)S(1)}, u32[]{:S(2)}, u32[]{:S(2)}) %collective-permute-start.1) | collective-permute-done | bytes 2097184 | tf_op jit(solution)/shard_map/while/body/eval_jaxpr/ppermute | solution.py:14
  40.9 4.1 %select_reduce_fusion.5 = f32[1024]{0:T(1024)S(1)} fusion(s32[1024]{0:T(1024)S(1)} %get-tuple-element.246, s32[1024]{0:T(1024)S(1)} %get-tuple-element.220, bf16[1024,1024]{1,0:T(8,128)(2,1)} %get-tuple-element.249, bf16[1024,1024]{1,0:T(8,128)(2,1)S(1)} %collective-permute-done.1), kind=kOutput, calls=%fused_computation.clone.1 | convolution fusion | flops 2150628352 | bytes 4206592 | tf_op jit(solution)/shard_map/while/body/eval_jaxpr/dot_general | solution.py:32
  45.0 0.0 collective-permute-done
  45.0 4.0 %select_reduce_fusion.6 = f32[1024]{0:T(1024)S(1)} fusion(s32[1024]{0:T(1024)S(1)} %get-tuple-element.246, s32[1024]{0:T(1024)S(1)} %get-tuple-element.221, bf16[1024,1024]{1,0:T(8,128)(2,1)S(1)} %copy-done.1, bf16[1024,1024]{1,0:T(8,128)(2,1)} %collective-permute-done), kind=kOutput, calls=%fused_computation.1.clone.1 | convolution fusion | flops 2150628352 | bytes 4206592 | tf_op jit(solution)/shard_map/while/body/eval_jaxpr/dot_general | solution.py:32
  49.0 1.3 copy.13
  50.4 3.1 %copy.12 = bf16[1024,1024]{1,0:T(8,128)(2,1)} copy(bf16[1024,1024]{1,0:T(8,128)(2,1)} %collective-permute-done) | data formatting | bytes 4194304 | tf_op jit(solution)/shard_map/while
  53.5 1.9 collective-permute-start.1
  55.4 7.9 %collective-permute-start = (bf16[1024,1024]{1,0:T(8,128)(2,1)}, bf16[1024,1024]{1,0:T(8,128)(2,1)}, u32[]{:S(2)}, u32[]{:S(2)}) collective-permute-start(bf16[1024,1024]{1,0:T(8,128)(2,1)} %get-tuple-element.233), channel_id=1, source_target_pairs={{1,0},{2,1},{3,2},{4,3},{5,4},{6,5},{7,6},{8,7},{9,8},{10,9},{11,1... | collective-permute-start | bytes 6291464 | tf_op jit(solution)/shard_map/while/body/eval_jaxpr/ppermute | solution.py:14
  63.3 0.1 slice.13
  63.4 0.6 convert_reduce_fusion.4
  64.0 21.2 %collective-permute-done.1 = bf16[1024,1024]{1,0:T(8,128)(2,1)S(1)} collective-permute-done((bf16[1024,1024]{1,0:T(8,128)(2,1)}, bf16[1024,1024]{1,0:T(8,128)(2,1)S(1)}, u32[]{:S(2)}, u32[]{:S(2)}) %collective-permute-start.1) | collective-permute-done | bytes 2097184 | tf_op jit(solution)/shard_map/while/body/eval_jaxpr/ppermute | solution.py:14
  85.2 4.1 %select_reduce_fusion.5 = f32[1024]{0:T(1024)S(1)} fusion(s32[1024]{0:T(1024)S(1)} %get-tuple-element.246, s32[1024]{0:T(1024)S(1)} %get-tuple-element.220, bf16[1024,1024]{1,0:T(8,128)(2,1)} %get-tuple-element.249, bf16[1024,1024]{1,0:T(8,128)(2,1)S(1)} %collective-permute-done.1), kind=kOutput, calls=%fused_computation.clone.1 | convolution fusion | flops 2150628352 | bytes 4206592 | tf_op jit(solution)/shard_map/while/body/eval_jaxpr/dot_general | solution.py:32
  89.4 4.0 %select_reduce_fusion.6 = f32[1024]{0:T(1024)S(1)} fusion(s32[1024]{0:T(1024)S(1)} %get-tuple-element.246, s32[1024]{0:T(1024)S(1)} %get-tuple-element.221, bf16[1024,1024]{1,0:T(8,128)(2,1)S(1)} %copy-done.1, bf16[1024,1024]{1,0:T(8,128)(2,1)} %collective-permute-done), kind=kOutput, calls=%fused_computation.1.clone.1 | convolution fusion | flops 2150628352 | bytes 4206592 | tf_op jit(solution)/shard_map/while/body/eval_jaxpr/dot_general | solution.py:32
  93.4 1.3 copy.13
  94.7 3.1 %copy.12 = bf16[1024,1024]{1,0:T(8,128)(2,1)} copy(bf16[1024,1024]{1,0:T(8,128)(2,1)} %collective-permute-done) | data formatting | bytes 4194304 | tf_op jit(solution)/shard_map/while
  97.8 1.9 collective-permute-start.1
  99.8 7.9 %collective-permute-start = (bf16[1024,1024]{1,0:T(8,128)(2,1)}, bf16[1024,1024]{1,0:T(8,128)(2,1)}, u32[]{:S(2)}, u32[]{:S(2)}) collective-permute-start(bf16[1024,1024]{1,0:T(8,128)(2,1)} %get-tuple-element.233), channel_id=1, source_target_pairs={{1,0},{2,1},{3,2},{4,3},{5,4},{6,5},{7,6},{8,7},{9,8},{10,9},{11,1... | collective-permute-start | bytes 6291464 | tf_op jit(solution)/shard_map/while/body/eval_jaxpr/ppermute | solution.py:14
  107.6 0.1 slice.13
  107.7 0.6 convert_reduce_fusion.4
  108.4 21.2 %collective-permute-done.1 = bf16[1024,1024]{1,0:T(8,128)(2,1)S(1)} collective-permute-done((bf16[1024,1024]{1,0:T(8,128)(2,1)}, bf16[1024,1024]{1,0:T(8,128)(2,1)S(1)}, u32[]{:S(2)}, u32[]{:S(2)}) %collective-permute-start.1) | collective-permute-done | bytes 2097184 | tf_op jit(solution)/shard_map/while/body/eval_jaxpr/ppermute | solution.py:14
  129.6 4.1 %select_reduce_fusion.5 = f32[1024]{0:T(1024)S(1)} fusion(s32[1024]{0:T(1024)S(1)} %get-tuple-element.246, s32[1024]{0:T(1024)S(1)} %get-tuple-element.220, bf16[1024,1024]{1,0:T(8,128)(2,1)} %get-tuple-element.249, bf16[1024,1024]{1,0:T(8,128)(2,1)S(1)} %collective-permute-done.1), kind=kOutput, calls=%fused_computation.clone.1 | convolution fusion | flops 2150628352 | bytes 4206592 | tf_op jit(solution)/shard_map/while/body/eval_jaxpr/dot_general | solution.py:32
  133.8 4.0 %select_reduce_fusion.6 = f32[1024]{0:T(1024)S(1)} fusion(s32[1024]{0:T(1024)S(1)} %get-tuple-element.246, s32[1024]{0:T(1024)S(1)} %get-tuple-element.221, bf16[1024,1024]{1,0:T(8,128)(2,1)S(1)} %copy-done.1, bf16[1024,1024]{1,0:T(8,128)(2,1)} %collective-permute-done), kind=kOutput, calls=%fused_computation.1.clone.1 | convolution fusion | flops 2150628352 | bytes 4206592 | tf_op jit(solution)/shard_map/while/body/eval_jaxpr/dot_general | solution.py:32
  137.8 1.3 copy.13
  139.1 3.1 %copy.12 = bf16[1024,1024]{1,0:T(8,128)(2,1)} copy(bf16[1024,1024]{1,0:T(8,128)(2,1)} %collective-permute-done) | data formatting | bytes 4194304 | tf_op jit(solution)/shard_map/while
  142.2 1.9 collective-permute-start.1
  144.1 7.9 %collective-permute-start = (bf16[1024,1024]{1,0:T(8,128)(2,1)}, bf16[1024,1024]{1,0:T(8,128)(2,1)}, u32[]{:S(2)}, u32[]{:S(2)}) collective-permute-start(bf16[1024,1024]{1,0:T(8,128)(2,1)} %get-tuple-element.233), channel_id=1, source_target_pairs={{1,0},{2,1},{3,2},{4,3},{5,4},{6,5},{7,6},{8,7},{9,8},{10,9},{11,1... | collective-permute-start | bytes 6291464 | tf_op jit(solution)/shard_map/while/body/eval_jaxpr/ppermute | solution.py:14
  152.0 0.1 slice.13
  152.1 0.6 convert_reduce_fusion.4
  152.7 21.2 %collective-permute-done.1 = bf16[1024,1024]{1,0:T(8,128)(2,1)S(1)} collective-permute-done((bf16[1024,1024]{1,0:T(8,128)(2,1)}, bf16[1024,1024]{1,0:T(8,128)(2,1)S(1)}, u32[]{:S(2)}, u32[]{:S(2)}) %collective-permute-start.1) | collective-permute-done | bytes 2097184 | tf_op jit(solution)/shard_map/while/body/eval_jaxpr/ppermute | solution.py:14
  174.0 4.1 %select_reduce_fusion.5 = f32[1024]{0:T(1024)S(1)} fusion(s32[1024]{0:T(1024)S(1)} %get-tuple-element.246, s32[1024]{0:T(1024)S(1)} %get-tuple-element.220, bf16[1024,1024]{1,0:T(8,128)(2,1)} %get-tuple-element.249, bf16[1024,1024]{1,0:T(8,128)(2,1)S(1)} %collective-permute-done.1), kind=kOutput, calls=%fused_computation.clone.1 | convolution fusion | flops 2150628352 | bytes 4206592 | tf_op jit(solution)/shard_map/while/body/eval_jaxpr/dot_general | solution.py:32
  178.1 4.0 %select_reduce_fusion.6 = f32[1024]{0:T(1024)S(1)} fusion(s32[1024]{0:T(1024)S(1)} %get-tuple-element.246, s32[1024]{0:T(1024)S(1)} %get-tuple-element.221, bf16[1024,1024]{1,0:T(8,128)(2,1)S(1)} %copy-done.1, bf16[1024,1024]{1,0:T(8,128)(2,1)} %collective-permute-done), kind=kOutput, calls=%fused_computation.1.clone.1 | convolution fusion | flops 2150628352 | bytes 4206592 | tf_op jit(solution)/shard_map/while/body/eval_jaxpr/dot_general | solution.py:32
  182.1 1.3 copy.13
  183.5 3.1 %copy.12 = bf16[1024,1024]{1,0:T(8,128)(2,1)} copy(bf16[1024,1024]{1,0:T(8,128)(2,1)} %collective-permute-done) | data formatting | bytes 4194304 | tf_op jit(solution)/shard_map/while
  186.5 1.9 collective-permute-start.1
  188.5 7.9 %collective-permute-start = (bf16[1024,1024]{1,0:T(8,128)(2,1)}, bf16[1024,1024]{1,0:T(8,128)(2,1)}, u32[]{:S(2)}, u32[]{:S(2)}) collective-permute-start(bf16[1024,1024]{1,0:T(8,128)(2,1)} %get-tuple-element.233), channel_id=1, source_target_pairs={{1,0},{2,1},{3,2},{4,3},{5,4},{6,5},{7,6},{8,7},{9,8},{10,9},{11,1... | collective-permute-start | bytes 6291464 | tf_op jit(solution)/shard_map/while/body/eval_jaxpr/ppermute | solution.py:14
  196.3 0.1 slice.13
  196.4 0.6 convert_reduce_fusion.4
  197.1 21.2 %collective-permute-done.1 = bf16[1024,1024]{1,0:T(8,128)(2,1)S(1)} collective-permute-done((bf16[1024,1024]{1,0:T(8,128)(2,1)}, bf16[1024,1024]{1,0:T(8,128)(2,1)S(1)}, u32[]{:S(2)}, u32[]{:S(2)}) %collective-permute-start.1) | collective-permute-done | bytes 2097184 | tf_op jit(solution)/shard_map/while/body/eval_jaxpr/ppermute | solution.py:14
  218.3 4.1 %select_reduce_fusion.5 = f32[1024]{0:T(1024)S(1)} fusion(s32[1024]{0:T(1024)S(1)} %get-tuple-element.246, s32[1024]{0:T(1024)S(1)} %get-tuple-element.220, bf16[1024,1024]{1,0:T(8,128)(2,1)} %get-tuple-element.249, bf16[1024,1024]{1,0:T(8,128)(2,1)S(1)} %collective-permute-done.1), kind=kOutput, calls=%fused_computation.clone.1 | convolution fusion | flops 2150628352 | bytes 4206592 | tf_op jit(solution)/shard_map/while/body/eval_jaxpr/dot_general | solution.py:32
  222.5 4.0 %select_reduce_fusion.6 = f32[1024]{0:T(1024)S(1)} fusion(s32[1024]{0:T(1024)S(1)} %get-tuple-element.246, s32[1024]{0:T(1024)S(1)} %get-tuple-element.221, bf16[1024,1024]{1,0:T(8,128)(2,1)S(1)} %copy-done.1, bf16[1024,1024]{1,0:T(8,128)(2,1)} %collective-permute-done), kind=kOutput, calls=%fused_computation.1.clone.1 | convolution fusion | flops 2150628352 | bytes 4206592 | tf_op jit(solution)/shard_map/while/body/eval_jaxpr/dot_general | solution.py:32
  226.5 1.3 copy.13
  227.8 3.1 %copy.12 = bf16[1024,1024]{1,0:T(8,128)(2,1)} copy(bf16[1024,1024]{1,0:T(8,128)(2,1)} %collective-permute-done) | data formatting | bytes 4194304 | tf_op jit(solution)/shard_map/while
  230.9 1.9 collective-permute-start.1
  232.8 7.9 %collective-permute-start = (bf16[1024,1024]{1,0:T(8,128)(2,1)}, bf16[1024,1024]{1,0:T(8,128)(2,1)}, u32[]{:S(2)}, u32[]{:S(2)}) collective-permute-start(bf16[1024,1024]{1,0:T(8,128)(2,1)} %get-tuple-element.233), channel_id=1, source_target_pairs={{1,0},{2,1},{3,2},{4,3},{5,4},{6,5},{7,6},{8,7},{9,8},{10,9},{11,1... | collective-permute-start | bytes 6291464 | tf_op jit(solution)/shard_map/while/body/eval_jaxpr/ppermute | solution.py:14
  240.7 0.1 slice.13
  240.8 0.6 convert_reduce_fusion.4
  241.4 21.2 %collective-permute-done.1 = bf16[1024,1024]{1,0:T(8,128)(2,1)S(1)} collective-permute-done((bf16[1024,1024]{1,0:T(8,128)(2,1)}, bf16[1024,1024]{1,0:T(8,128)(2,1)S(1)}, u32[]{:S(2)}, u32[]{:S(2)}) %collective-permute-start.1) | collective-permute-done | bytes 2097184 | tf_op jit(solution)/shard_map/while/body/eval_jaxpr/ppermute | solution.py:14
  262.7 4.1 %select_reduce_fusion.5 = f32[1024]{0:T(1024)S(1)} fusion(s32[1024]{0:T(1024)S(1)} %get-tuple-element.246, s32[1024]{0:T(1024)S(1)} %get-tuple-element.220, bf16[1024,1024]{1,0:T(8,128)(2,1)} %get-tuple-element.249, bf16[1024,1024]{1,0:T(8,128)(2,1)S(1)} %collective-permute-done.1), kind=kOutput, calls=%fused_computation.clone.1 | convolution fusion | flops 2150628352 | bytes 4206592 | tf_op jit(solution)/shard_map/while/body/eval_jaxpr/dot_general | solution.py:32
  266.8 4.0 %select_reduce_fusion.6 = f32[1024]{0:T(1024)S(1)} fusion(s32[1024]{0:T(1024)S(1)} %get-tuple-element.246, s32[1024]{0:T(1024)S(1)} %get-tuple-element.221, bf16[1024,1024]{1,0:T(8,128)(2,1)S(1)} %copy-done.1, bf16[1024,1024]{1,0:T(8,128)(2,1)} %collective-permute-done), kind=kOutput, calls=%fused_computation.1.clone.1 | convolution fusion | flops 2150628352 | bytes 4206592 | tf_op jit(solution)/shard_map/while/body/eval_jaxpr/dot_general | solution.py:32
  270.8 1.3 copy.13
  272.2 3.1 %copy.12 = bf16[1024,1024]{1,0:T(8,128)(2,1)} copy(bf16[1024,1024]{1,0:T(8,128)(2,1)} %collective-permute-done) | data formatting | bytes 4194304 | tf_op jit(solution)/shard_map/while
  275.3 0.6 copy-done.3
  (51 shorter events, 0.2 us)
Async XLA Ops:
  0.0 3.4 %copy-start.2 = (bf16[1024,1024]{1,0:T(8,128)(2,1)S(1)}, bf16[1024,1024]{1,0:T(8,128)(2,1)}, u32[]{:S(2)}) copy-start(bf16[1024,1024]{1,0:T(8,128)(2,1)} %param.4) | copy-start | bytes 6291460
  3.8 4.0 %copy-start = (bf16[1024,1024]{1,0:T(8,128)(2,1)}, bf16[1024,1024]{1,0:T(8,128)(2,1)S(1)}, u32[]{:S(2)}) copy-start(bf16[1024,1024]{1,0:T(8,128)(2,1)S(1)} %fusion.1) | copy-start | bytes 6291460
  7.8 1.3 copy-start.4
  9.1 31.8 %collective-permute-start.1 = (bf16[1024,1024]{1,0:T(8,128)(2,1)}, bf16[1024,1024]{1,0:T(8,128)(2,1)S(1)}, u32[]{:S(2)}, u32[]{:S(2)}) collective-permute-start(bf16[1024,1024]{1,0:T(8,128)(2,1)} %get-tuple-element.234), channel_id=1, source_target_pairs={{0,1},{1,2},{2,3},{3,4},{4,5},{5,6},{6,7},{7,8},{8,9},{9,10},{10,1... | collective-permute-start | bytes 6291464 | tf_op jit(solution)/shard_map/while/body/eval_jaxpr/ppermute | solution.py:14
  11.0 34.0 %collective-permute-start = (bf16[1024,1024]{1,0:T(8,128)(2,1)}, bf16[1024,1024]{1,0:T(8,128)(2,1)}, u32[]{:S(2)}, u32[]{:S(2)}) collective-permute-start(bf16[1024,1024]{1,0:T(8,128)(2,1)} %get-tuple-element.233), channel_id=1, source_target_pairs={{1,0},{2,1},{3,2},{4,3},{5,4},{6,5},{7,6},{8,7},{9,8},{10,9},{11,1... | collective-permute-start | bytes 6291464 | tf_op jit(solution)/shard_map/while/body/eval_jaxpr/ppermute | solution.py:14
  40.9 4.1 %copy-start.1 = (bf16[1024,1024]{1,0:T(8,128)(2,1)S(1)}, bf16[1024,1024]{1,0:T(8,128)(2,1)}, u32[]{:S(2)}) copy-start(bf16[1024,1024]{1,0:T(8,128)(2,1)} %get-tuple-element.249) | copy-start | bytes 6291460 | tf_op jit(solution)/shard_map/while
  53.5 31.8 %collective-permute-start.1 = (bf16[1024,1024]{1,0:T(8,128)(2,1)}, bf16[1024,1024]{1,0:T(8,128)(2,1)S(1)}, u32[]{:S(2)}, u32[]{:S(2)}) collective-permute-start(bf16[1024,1024]{1,0:T(8,128)(2,1)} %get-tuple-element.234), channel_id=1, source_target_pairs={{0,1},{1,2},{2,3},{3,4},{4,5},{5,6},{6,7},{7,8},{8,9},{9,10},{10,1... | collective-permute-start | bytes 6291464 | tf_op jit(solution)/shard_map/while/body/eval_jaxpr/ppermute | solution.py:14
  55.4 34.0 %collective-permute-start = (bf16[1024,1024]{1,0:T(8,128)(2,1)}, bf16[1024,1024]{1,0:T(8,128)(2,1)}, u32[]{:S(2)}, u32[]{:S(2)}) collective-permute-start(bf16[1024,1024]{1,0:T(8,128)(2,1)} %get-tuple-element.233), channel_id=1, source_target_pairs={{1,0},{2,1},{3,2},{4,3},{5,4},{6,5},{7,6},{8,7},{9,8},{10,9},{11,1... | collective-permute-start | bytes 6291464 | tf_op jit(solution)/shard_map/while/body/eval_jaxpr/ppermute | solution.py:14
  85.2 4.1 %copy-start.1 = (bf16[1024,1024]{1,0:T(8,128)(2,1)S(1)}, bf16[1024,1024]{1,0:T(8,128)(2,1)}, u32[]{:S(2)}) copy-start(bf16[1024,1024]{1,0:T(8,128)(2,1)} %get-tuple-element.249) | copy-start | bytes 6291460 | tf_op jit(solution)/shard_map/while
  97.8 31.8 %collective-permute-start.1 = (bf16[1024,1024]{1,0:T(8,128)(2,1)}, bf16[1024,1024]{1,0:T(8,128)(2,1)S(1)}, u32[]{:S(2)}, u32[]{:S(2)}) collective-permute-start(bf16[1024,1024]{1,0:T(8,128)(2,1)} %get-tuple-element.234), channel_id=1, source_target_pairs={{0,1},{1,2},{2,3},{3,4},{4,5},{5,6},{6,7},{7,8},{8,9},{9,10},{10,1... | collective-permute-start | bytes 6291464 | tf_op jit(solution)/shard_map/while/body/eval_jaxpr/ppermute | solution.py:14
  99.8 34.0 %collective-permute-start = (bf16[1024,1024]{1,0:T(8,128)(2,1)}, bf16[1024,1024]{1,0:T(8,128)(2,1)}, u32[]{:S(2)}, u32[]{:S(2)}) collective-permute-start(bf16[1024,1024]{1,0:T(8,128)(2,1)} %get-tuple-element.233), channel_id=1, source_target_pairs={{1,0},{2,1},{3,2},{4,3},{5,4},{6,5},{7,6},{8,7},{9,8},{10,9},{11,1... | collective-permute-start | bytes 6291464 | tf_op jit(solution)/shard_map/while/body/eval_jaxpr/ppermute | solution.py:14
  129.6 4.1 %copy-start.1 = (bf16[1024,1024]{1,0:T(8,128)(2,1)S(1)}, bf16[1024,1024]{1,0:T(8,128)(2,1)}, u32[]{:S(2)}) copy-start(bf16[1024,1024]{1,0:T(8,128)(2,1)} %get-tuple-element.249) | copy-start | bytes 6291460 | tf_op jit(solution)/shard_map/while
  142.2 31.8 %collective-permute-start.1 = (bf16[1024,1024]{1,0:T(8,128)(2,1)}, bf16[1024,1024]{1,0:T(8,128)(2,1)S(1)}, u32[]{:S(2)}, u32[]{:S(2)}) collective-permute-start(bf16[1024,1024]{1,0:T(8,128)(2,1)} %get-tuple-element.234), channel_id=1, source_target_pairs={{0,1},{1,2},{2,3},{3,4},{4,5},{5,6},{6,7},{7,8},{8,9},{9,10},{10,1... | collective-permute-start | bytes 6291464 | tf_op jit(solution)/shard_map/while/body/eval_jaxpr/ppermute | solution.py:14
  144.1 34.0 %collective-permute-start = (bf16[1024,1024]{1,0:T(8,128)(2,1)}, bf16[1024,1024]{1,0:T(8,128)(2,1)}, u32[]{:S(2)}, u32[]{:S(2)}) collective-permute-start(bf16[1024,1024]{1,0:T(8,128)(2,1)} %get-tuple-element.233), channel_id=1, source_target_pairs={{1,0},{2,1},{3,2},{4,3},{5,4},{6,5},{7,6},{8,7},{9,8},{10,9},{11,1... | collective-permute-start | bytes 6291464 | tf_op jit(solution)/shard_map/while/body/eval_jaxpr/ppermute | solution.py:14
  174.0 4.1 %copy-start.1 = (bf16[1024,1024]{1,0:T(8,128)(2,1)S(1)}, bf16[1024,1024]{1,0:T(8,128)(2,1)}, u32[]{:S(2)}) copy-start(bf16[1024,1024]{1,0:T(8,128)(2,1)} %get-tuple-element.249) | copy-start | bytes 6291460 | tf_op jit(solution)/shard_map/while
  186.5 31.8 %collective-permute-start.1 = (bf16[1024,1024]{1,0:T(8,128)(2,1)}, bf16[1024,1024]{1,0:T(8,128)(2,1)S(1)}, u32[]{:S(2)}, u32[]{:S(2)}) collective-permute-start(bf16[1024,1024]{1,0:T(8,128)(2,1)} %get-tuple-element.234), channel_id=1, source_target_pairs={{0,1},{1,2},{2,3},{3,4},{4,5},{5,6},{6,7},{7,8},{8,9},{9,10},{10,1... | collective-permute-start | bytes 6291464 | tf_op jit(solution)/shard_map/while/body/eval_jaxpr/ppermute | solution.py:14
  188.5 34.0 %collective-permute-start = (bf16[1024,1024]{1,0:T(8,128)(2,1)}, bf16[1024,1024]{1,0:T(8,128)(2,1)}, u32[]{:S(2)}, u32[]{:S(2)}) collective-permute-start(bf16[1024,1024]{1,0:T(8,128)(2,1)} %get-tuple-element.233), channel_id=1, source_target_pairs={{1,0},{2,1},{3,2},{4,3},{5,4},{6,5},{7,6},{8,7},{9,8},{10,9},{11,1... | collective-permute-start | bytes 6291464 | tf_op jit(solution)/shard_map/while/body/eval_jaxpr/ppermute | solution.py:14
  218.3 4.1 %copy-start.1 = (bf16[1024,1024]{1,0:T(8,128)(2,1)S(1)}, bf16[1024,1024]{1,0:T(8,128)(2,1)}, u32[]{:S(2)}) copy-start(bf16[1024,1024]{1,0:T(8,128)(2,1)} %get-tuple-element.249) | copy-start | bytes 6291460 | tf_op jit(solution)/shard_map/while
  230.9 31.8 %collective-permute-start.1 = (bf16[1024,1024]{1,0:T(8,128)(2,1)}, bf16[1024,1024]{1,0:T(8,128)(2,1)S(1)}, u32[]{:S(2)}, u32[]{:S(2)}) collective-permute-start(bf16[1024,1024]{1,0:T(8,128)(2,1)} %get-tuple-element.234), channel_id=1, source_target_pairs={{0,1},{1,2},{2,3},{3,4},{4,5},{5,6},{6,7},{7,8},{8,9},{9,10},{10,1... | collective-permute-start | bytes 6291464 | tf_op jit(solution)/shard_map/while/body/eval_jaxpr/ppermute | solution.py:14
  232.8 34.0 %collective-permute-start = (bf16[1024,1024]{1,0:T(8,128)(2,1)}, bf16[1024,1024]{1,0:T(8,128)(2,1)}, u32[]{:S(2)}, u32[]{:S(2)}) collective-permute-start(bf16[1024,1024]{1,0:T(8,128)(2,1)} %get-tuple-element.233), channel_id=1, source_target_pairs={{1,0},{2,1},{3,2},{4,3},{5,4},{6,5},{7,6},{8,7},{9,8},{10,9},{11,1... | collective-permute-start | bytes 6291464 | tf_op jit(solution)/shard_map/while/body/eval_jaxpr/ppermute | solution.py:14
  262.7 4.1 %copy-start.1 = (bf16[1024,1024]{1,0:T(8,128)(2,1)S(1)}, bf16[1024,1024]{1,0:T(8,128)(2,1)}, u32[]{:S(2)}) copy-start(bf16[1024,1024]{1,0:T(8,128)(2,1)} %get-tuple-element.249) | copy-start | bytes 6291460 | tf_op jit(solution)/shard_map/while
  275.3 0.6 copy-start.3
where the time goes:
time: 277 us; the launch traced here: 276 us
  waiting for transfers between devices  127 us (46%)
  starting transfers between devices  58.6 us (21%)
  matrix products  51.2 us (18%)
  local copies, waits for them, and re-layouts  31.2 us (11%)
  other arithmetic  6.76 us (2%)
    ppermute x12, waiting for transfers between devices, shifted(): return lax.ppermute(block, axis, route)  127 us
    ppermute x12, starting transfers between devices, shifted(): return lax.ppermute(block, axis, route)  58.6 us
    dot_general x13, matrix products, pair_tile(): lax.dot_general(left_rows, right_rows, (((1,), (1,)), ((), ())), preferre...  51.2 us
    while x24, local copies, waits for them, and re-layouts  26.6 us
  transfers between devices with their start and end apart: 12, of which 6 were waited for; matrix products, arithmetic and copies ran while one was open for 11% of the time, Pallas kernels for 0%

commit v1 on v0

v1 whole, which is shorter than its diff:
```python
import math

import jax
import jax.numpy as jnp
from jax import lax
from jax.sharding import PartitionSpec as P

AXES = ("grp", "work")


def permuted(block, target):
    count = lax.axis_size(AXES)
    return lax.ppermute(block, AXES, [(i, target(i) % count) for i in range(count)])


def to_unit(values):
    widened = values.astype(jnp.float32)
    factor = lax.rsqrt(jnp.mean(widened * widened, axis=1, keepdims=True) + 1e-06) / math.sqrt(
        values.shape[1]
    )
    return (widened * factor).astype(jnp.bfloat16)


def cluster_of(offsets, first_row, row_count):
    row_index = first_row + jnp.arange(row_count, dtype=jnp.int32)
    return jnp.sum((offsets[None, 1:] <= row_index[:, None]).astype(jnp.int32), axis=1)


def pair_tile(left_rows, right_rows, left_ids, right_ids, same_block=False):
    scores = lax.dot_general(
        left_rows, right_rows, (((1,), (1,)), ((), ())), preferred_element_type=jnp.float32
    )
    same_cluster = left_ids[:, None] == right_ids[None, :]
    if same_block:
        positions = jnp.arange(left_ids.shape[0], dtype=jnp.int32)
        same_cluster = same_cluster & (positions[:, None] != positions[None, :])
    masked = jnp.where(same_cluster, scores, -1.0)
    return (jnp.max(masked, axis=1), jnp.max(masked, axis=0))


def shards(embeddings, offsets):
    row_count = embeddings.shape[0]
    count = lax.axis_size(AXES)
    me = lax.axis_index(AXES)
    core = me % 2

    def ids_of(device):
        return cluster_of(offsets, (device % count) * row_count, row_count)

    own = to_unit(embeddings)
    near = permuted(own, lambda i: i - 2)
    far = permuted(own, lambda i: i - 6)
    near_other = permuted(near, lambda i: i ^ 1)
    extra = permuted(jnp.where(core == 1, own, far), lambda i: i ^ 1)
    other = me + 1 - 2 * core
    own_ids, near_ids, far_ids = ids_of(me), ids_of(me + 2), ids_of(me + 6)
    near_other_ids = ids_of(other + 2)
    extra_ids = ids_of(jnp.where(core == 1, other + 6, other))

    best = pair_tile(own, own, own_ids, own_ids, True)[0]
    row, near_best = pair_tile(own, near, own_ids, near_ids)
    best = jnp.maximum(best, row)
    row, far_best = pair_tile(own, far, own_ids, far_ids)
    best = jnp.maximum(best, row)
    row, near_other_best = pair_tile(own, near_other, own_ids, near_other_ids)
    best = jnp.maximum(best, row)
    row, extra_best = pair_tile(own, extra, own_ids, extra_ids)
    best = jnp.maximum(best, row)
    row, column = pair_tile(far, near, far_ids, near_ids)
    far_best, near_best = jnp.maximum(far_best, row), jnp.maximum(near_best, column)
    row, column = pair_tile(far, near_other, far_ids, near_other_ids)
    far_best, near_other_best = jnp.maximum(far_best, row), jnp.maximum(near_other_best, column)
    best = jnp.maximum(best, permuted(near_best, lambda i: i + 2))
    best = jnp.maximum(best, permuted(near_other_best, lambda i: (i ^ 1) + 2))
    best = jnp.maximum(best, permuted(far_best, lambda i: i + 6))
    best = jnp.maximum(best, permuted(extra_best, lambda i: i + 1 if i % 2 == 0 else i + 5))
    return best


def solution(mesh):
    return jax.shard_map(
        shards,
        mesh=mesh,
        in_specs=(P(AXES, None), P()),
        out_specs=P(AXES),
        check_vma=False,
    )
```

time: 277 us -> 148 us (0.53)
  the two profiles are of different devices: /device:TPU:64 before, /device:TPU:1 now
where the time goes in v1:
time: 148 us; the launch traced here: 147 us
  waiting for transfers between devices  67.5 us (46%)
  starting transfers between devices  38.2 us (26%)
  matrix products  33.6 us (23%)
  other arithmetic  7.1 us (5%)
    ppermute x8, waiting for transfers between devices, permuted(): lax.ppermute(block, AXES, [(i, target(i) % count) for i in range(count)])  67.5 us
    ppermute x8, starting transfers between devices, permuted(): lax.ppermute(block, AXES, [(i, target(i) % count) for i in range(count)])  38.2 us
    dot_general x7, matrix products, pair_tile(): lax.dot_general(left_rows, right_rows, (((1,), (1,)), ((), ())), preferre...  33.6 us
  transfers between devices with their start and end apart: 8, of which 3 were waited for; matrix products, arithmetic and copies ran while one was open for 17% of the time, Pallas kernels for 0%

profile of v1, /device:TPU:1, one launch (start us, length us, event | category | flops | bytes accessed | tf_op | source)
XLA Modules:
  0.0 146.7 jit_solution(613429669703751893)
XLA Ops:
  0.0 0.0 copy-start
  0.0 2.2 %fusion = f32[1024]{0:T(1024)S(1)} fusion(bf16[1024,1024]{1,0:T(8,128)(2,1)} %param.2), kind=kLoop, calls=%fused_computation.2 | loop fusion | flops 3144704 | bytes 2101248 | tf_op jit(solution)/shard_map/reduce_sum | solution.py:18
  2.2 0.0 copy-done
  2.2 0.0 copy-start.1
  2.3 1.8 %fusion.1 = bf16[1024,1024]{1,0:T(8,128)(2,1)} fusion(bf16[1024,1024]{1,0:T(8,128)(2,1)S(1)} %copy-done, f32[1024]{0:T(1024)S(1)} %rsqrt_multiply_fusion), kind=kLoop, calls=%fused_computation.3 | loop fusion | flops 3145728 | bytes 4198400 | tf_op jit(solution)/shard_map/convert_element_type | solution.py:21
  4.0 8.0 %collective-permute-start.1 = (bf16[1024,1024]{1,0:T(8,128)(2,1)}, bf16[1024,1024]{1,0:T(8,128)(2,1)}, u32[]{:S(2)}, u32[]{:S(2)}) collective-permute-start(bf16[1024,1024]{1,0:T(8,128)(2,1)} %fusion.1), channel_id=1, source_target_pairs={{0,122},{1,123},{2,124},{3,125},{4,126},{5,127},{6,0},{7,1},{8,2},... | collective-permute-start | bytes 6291464 | tf_op jit(solution)/shard_map/ppermute | solution.py:13
  12.0 1.5 collective-permute-start
  13.4 0.0 copy-done.1
  13.4 0.1 slice.2
  13.5 43.1 %collective-permute-done.1 = bf16[1024,1024]{1,0:T(8,128)(2,1)} collective-permute-done((bf16[1024,1024]{1,0:T(8,128)(2,1)}, bf16[1024,1024]{1,0:T(8,128)(2,1)}, u32[]{:S(2)}, u32[]{:S(2)}) %collective-permute-start.1) | collective-permute-done | bytes 2097184 | tf_op jit(solution)/shard_map/ppermute | solution.py:13
  56.6 0.7 broadcast_select_fusion
  57.3 3.2 %collective-permute-start.3 = (bf16[1024,1024]{1,0:T(8,128)(2,1)S(1)}, bf16[1024,1024]{1,0:T(8,128)(2,1)S(1)}, u32[]{:S(2)}, u32[]{:S(2)}) collective-permute-start(bf16[1024,1024]{1,0:T(8,128)(2,1)S(1)} %broadcast_select_fusion), channel_id=1, source_target_pairs={{0,1},{1,0},{2,3},{3,2},{4,5},{5,4},{6,7},{7,6},{8,9},{9,8},{10,11... | collective-permute-start | bytes 6291464 | tf_op jit(solution)/shard_map/ppermute | solution.py:13
  60.5 1.8 %convert_reduce_fusion.3 = (s32[1024]{0:T(1024)S(1)}, s32[1024]{0:T(1024)S(1)}, s32[1024]{0:T(1024)S(1)}, s32[1024]{0:T(1024)S(1)}, s32[1024]{0:T(1024)S(1)}) fusion(s32[256]{0:T(256)S(1)} %slice.2, s32[1024]{0:T(1024)S(1)} %get-tuple-element.35, s32[1024]{0:T(1024)S(1)} %get-tuple-element.34, s32[1024]{0:T(1024)S(1)} %get-tuple-element.33, ...), kind=kLoop, calls=%fused_computation.29 | loop fusion | flops 3927040 | bytes 41984 | tf_op jit(solution)/shard_map/reduce_sum | solution.py:26
  62.3 23.1 %collective-permute-done = bf16[1024,1024]{1,0:T(8,128)(2,1)} collective-permute-done((bf16[1024,1024]{1,0:T(8,128)(2,1)}, bf16[1024,1024]{1,0:T(8,128)(2,1)}, u32[]{:S(2)}, u32[]{:S(2)}) %collective-permute-start) | collective-permute-done | bytes 2097184 | tf_op jit(solution)/shard_map/ppermute | solution.py:13
  85.4 2.7 %collective-permute-start.2 = (bf16[1024,1024]{1,0:T(8,128)(2,1)}, bf16[1024,1024]{1,0:T(8,128)(2,1)S(1)}, u32[]{:S(2)}, u32[]{:S(2)}) collective-permute-start(bf16[1024,1024]{1,0:T(8,128)(2,1)} %collective-permute-done), channel_id=1, source_target_pairs={{0,1},{1,0},{2,3},{3,2},{4,5},{5,4},{6,7},{7,6},{8,9},{9,8},{10,11... | collective-permute-start | bytes 6291464 | tf_op jit(solution)/shard_map/ppermute | solution.py:13
  88.1 4.6 %fusion.19 = f32[1024,1024]{0,1:T(8,128)S(1)} fusion(bf16[1024,1024]{1,0:T(8,128)(2,1)} %collective-permute-done.1, bf16[1024,1024]{1,0:T(8,128)(2,1)} %collective-permute-done), kind=kOutput, calls=%fused_computation.43 | convolution fusion | flops 2147483648 | bytes 8388608 | tf_op jit(solution)/shard_map/dot_general | solution.py:30
  92.7 4.6 %fusion.15 = f32[1024,1024]{0,1:T(8,128)S(1)} fusion(bf16[1024,1024]{1,0:T(8,128)(2,1)} %fusion.1, bf16[1024,1024]{1,0:T(8,128)(2,1)} %collective-permute-done), kind=kOutput, calls=%fused_computation.39 | convolution fusion | flops 2147483648 | bytes 8388608 | tf_op jit(solution)/shard_map/dot_general | solution.py:30
  97.3 4.6 %fusion.16 = f32[1024,1024]{0,1:T(8,128)S(1)} fusion(bf16[1024,1024]{1,0:T(8,128)(2,1)} %fusion.1, bf16[1024,1024]{1,0:T(8,128)(2,1)} %collective-permute-done.1), kind=kOutput, calls=%fused_computation.40 | convolution fusion | flops 2147483648 | bytes 8388608 | tf_op jit(solution)/shard_map/dot_general | solution.py:30
  101.9 0.0 collective-permute-done.3
  101.9 4.0 %fusion.18 = f32[1024,1024]{0,1:T(8,128)S(1)} fusion(bf16[1024,1024]{1,0:T(8,128)(2,1)} %fusion.1, bf16[1024,1024]{1,0:T(8,128)(2,1)S(1)} %collective-permute-done.3), kind=kOutput, calls=%fused_computation.42 | convolution fusion | flops 2147483648 | bytes 8388608 | tf_op jit(solution)/shard_map/dot_general | solution.py:30
  105.9 0.0 collective-permute-done.2
  105.9 4.0 %fusion.17 = f32[1024,1024]{0,1:T(8,128)S(1)} fusion(bf16[1024,1024]{1,0:T(8,128)(2,1)} %fusion.1, bf16[1024,1024]{1,0:T(8,128)(2,1)S(1)} %collective-permute-done.2), kind=kOutput, calls=%fused_computation.41 | convolution fusion | flops 2147483648 | bytes 8388608 | tf_op jit(solution)/shard_map/dot_general | solution.py:30
  109.9 7.1 %fusion.4 = (f32[1024]{0:T(1024)S(1)}, f32[1024]{0:T(1024)S(1)}, f32[1024]{0:T(1024)S(1)}, f32[1024]{0:T(1024)S(1)}, f32[1024]{0:T(1024)S(1)}, /*index=5*/f32[10...) fusion(f32[1024,1024]{0,1:T(8,128)S(1)} %fusion.15, ...), kind=kOutput, calls=%fused_computation.14 | convolution fusion | flops 2172637184 | bytes 25235456 | tf_op jit(solution)/shard_map/dot_general | solution.py:30
  117.0 0.3 collective-permute-start.5
  117.3 17.9 %collective-permute-start.6 = (f32[1024]{0:T(1024)S(1)}, f32[1024]{0:T(1024)S(1)}, u32[]{:S(2)}, u32[]{:S(2)}) collective-permute-start(f32[1024]{0:T(1024)S(1)} %maximum_maximum_fusion.1), channel_id=1, source_target_pairs={{0,6},{1,7},{2,8},{3,9},{4,10},{5,11},{6,12},{7,13},{8,14},{9,15},... | collective-permute-start | bytes 12296 | tf_op jit(solution)/shard_map/ppermute | solution.py:13
  135.3 4.0 %collective-permute-start.4 = (f32[1024]{0:T(1024)S(1)}, f32[1024]{0:T(1024)S(1)}, u32[]{:S(2)}, u32[]{:S(2)}) collective-permute-start(f32[1024]{0:T(1024)S(1)} %max.40), channel_id=1, source_target_pairs={{0,2},{1,3},{2,4},{3,5},{4,6},{5,7},{6,8},{7,9},{8,10},{9,11},{10,... | collective-permute-start | bytes 12296 | tf_op jit(solution)/shard_map/ppermute | solution.py:13
  139.2 0.6 collective-permute-start.7
  139.9 4.8 %select_reduce_fusion = f32[1024]{0:T(1024)S(1)} fusion(s32[1024]{0:T(1024)S(1)} %get-tuple-element.31, bf16[1024,1024]{1,0:T(8,128)(2,1)} %fusion.1), kind=kOutput, calls=%fused_computation.4 | convolution fusion | flops 2152725504 | bytes 2105344 | tf_op jit(solution)/shard_map/dot_general | solution.py:30
  144.7 1.3 collective-permute-done.5
  146.1 0.0 collective-permute-done.6
  146.1 0.0 collective-permute-done.4
  146.1 0.0 collective-permute-done.7
  146.1 0.6 maximum_maximum_fusion
  (7 shorter events, 0.0 us)
Async XLA Ops:
  0.0 2.2 %copy-start = (bf16[1024,1024]{1,0:T(8,128)(2,1)S(1)}, bf16[1024,1024]{1,0:T(8,128)(2,1)}, u32[]{:S(2)}) copy-start(bf16[1024,1024]{1,0:T(8,128)(2,1)} %param.2) | copy-start | bytes 6291460
  2.2 11.2 %copy-start.1 = (s32[257]{0:T(512)S(1)}, s32[257]{0:T(512)}, u32[]{:S(2)}) copy-start(s32[257]{0:T(512)} %param.3) | copy-start | bytes 3088
  4.0 52.6 %collective-permute-start.1 = (bf16[1024,1024]{1,0:T(8,128)(2,1)}, bf16[1024,1024]{1,0:T(8,128)(2,1)}, u32[]{:S(2)}, u32[]{:S(2)}) collective-permute-start(bf16[1024,1024]{1,0:T(8,128)(2,1)} %fusion.1), channel_id=1, source_target_pairs={{0,122},{1,123},{2,124},{3,125},{4,126},{5,127},{6,0},{7,1},{8,2},... | collective-permute-start | bytes 6291464 | tf_op jit(solution)/shard_map/ppermute | solution.py:13
  12.0 73.4 %collective-permute-start = (bf16[1024,1024]{1,0:T(8,128)(2,1)}, bf16[1024,1024]{1,0:T(8,128)(2,1)}, u32[]{:S(2)}, u32[]{:S(2)}) collective-permute-start(bf16[1024,1024]{1,0:T(8,128)(2,1)} %fusion.1), channel_id=1, source_target_pairs={{0,126},{1,127},{2,0},{3,1},{4,2},{5,3},{6,4},{7,5},{8,6},{9,7},{1... | collective-permute-start | bytes 6291464 | tf_op jit(solution)/shard_map/ppermute | solution.py:13
  57.3 44.6 %collective-permute-start.3 = (bf16[1024,1024]{1,0:T(8,128)(2,1)S(1)}, bf16[1024,1024]{1,0:T(8,128)(2,1)S(1)}, u32[]{:S(2)}, u32[]{:S(2)}) collective-permute-start(bf16[1024,1024]{1,0:T(8,128)(2,1)S(1)} %broadcast_select_fusion), channel_id=1, source_target_pairs={{0,1},{1,0},{2,3},{3,2},{4,5},{5,4},{6,7},{7,6},{8,9},{9,8},{10,11... | collective-permute-start | bytes 6291464 | tf_op jit(solution)/shard_map/ppermute | solution.py:13
  85.4 20.5 %collective-permute-start.2 = (bf16[1024,1024]{1,0:T(8,128)(2,1)}, bf16[1024,1024]{1,0:T(8,128)(2,1)S(1)}, u32[]{:S(2)}, u32[]{:S(2)}) collective-permute-start(bf16[1024,1024]{1,0:T(8,128)(2,1)} %collective-permute-done), channel_id=1, source_target_pairs={{0,1},{1,0},{2,3},{3,2},{4,5},{5,4},{6,7},{7,6},{8,9},{9,8},{10,11... | collective-permute-start | bytes 6291464 | tf_op jit(solution)/shard_map/ppermute | solution.py:13
  117.0 29.1 %collective-permute-start.5 = (f32[1024]{0:T(1024)S(1)}, f32[1024]{0:T(1024)S(1)}, u32[]{:S(2)}, u32[]{:S(2)}) collective-permute-start(f32[1024]{0:T(1024)S(1)} %max.42), channel_id=1, source_target_pairs={{0,3},{1,2},{2,5},{3,4},{4,7},{5,6},{6,9},{7,8},{8,11},{9,10},{10,... | collective-permute-start | bytes 12296 | tf_op jit(solution)/shard_map/ppermute | solution.py:13
  117.3 28.7 %collective-permute-start.6 = (f32[1024]{0:T(1024)S(1)}, f32[1024]{0:T(1024)S(1)}, u32[]{:S(2)}, u32[]{:S(2)}) collective-permute-start(f32[1024]{0:T(1024)S(1)} %maximum_maximum_fusion.1), channel_id=1, source_target_pairs={{0,6},{1,7},{2,8},{3,9},{4,10},{5,11},{6,12},{7,13},{8,14},{9,15},... | collective-permute-start | bytes 12296 | tf_op jit(solution)/shard_map/ppermute | solution.py:13
  135.3 10.8 %collective-permute-start.4 = (f32[1024]{0:T(1024)S(1)}, f32[1024]{0:T(1024)S(1)}, u32[]{:S(2)}, u32[]{:S(2)}) collective-permute-start(f32[1024]{0:T(1024)S(1)} %max.40), channel_id=1, source_target_pairs={{0,2},{1,3},{2,4},{3,5},{4,6},{5,7},{6,8},{7,9},{8,10},{9,11},{10,... | collective-permute-start | bytes 12296 | tf_op jit(solution)/shard_map/ppermute | solution.py:13
  139.2 6.8 %collective-permute-start.7 = (f32[1024]{0:T(1024)S(1)}, f32[1024]{0:T(1024)S(1)}, u32[]{:S(2)}, u32[]{:S(2)}) collective-permute-start(f32[1024]{0:T(1024)S(1)} %get-tuple-element.25), channel_id=1, source_target_pairs={{0,1},{1,6},{2,3},{3,8},{4,5},{5,10},{6,7},{7,12},{8,9},{9,14},{10... | collective-permute-start | bytes 12296 | tf_op jit(solution)/shard_map/ppermute | solution.py:13

commit v2 on v0

v2 whole, which is shorter than its diff:
```python
import jax
import jax.numpy as jnp
from jax import lax
from jax.experimental import pallas as pl
from jax.experimental.pallas import tpu as pltpu
from jax.sharding import PartitionSpec as P

AXES = ("grp", "work")
MESH = pl.DeviceIdType.MESH
ROWS = 1024
WIDTH = 1024
STEPS = 8
CHUNK = ROWS // STEPS
PIECES = 4
PIECE = CHUNK // PIECES
CHIPS = 64
DEVICES = 2 * CHIPS
LANES = 128


def dot(left, right):
    return lax.dot_general(
        left, right, (((1,), (1,)), ((), ())), preferred_element_type=jnp.float32
    )


def kernel(
    emb, offs, out,
    raw, own, relay, near, far,
    id_own, id_far, lane_own, lane_near, lane_far, table,
    row_own, row_far, col_near, col_far, reply, heard,
    raw_sem, near_s, far_s, hop_s, swap_s, extra_s, reply_s,
    relay_r, near_r, swap_r, far_r, extra_r, reply_r,
):
    grp = lax.axis_index("grp")
    work = lax.axis_index("work")
    core = work % 2
    x = (work // 2) % 4
    chip = grp * 16 + work // 2
    me = chip * 2 + core

    def device(distance, which):
        target = (chip + distance + CHIPS) % CHIPS
        return (target // 16, (target % 16) * 2 + which)

    partner = device(0, 1 - core)

    def remote(src, dst, send, recv, target):
        return pltpu.make_async_remote_copy(
            src_ref=src, dst_ref=dst, send_sem=send, recv_sem=recv,
            device_id=target, device_id_type=MESH,
        )

    barrier = pltpu.get_barrier_semaphore()

    def greet(target):
        pl.semaphore_signal(barrier, inc=1, device_id=target, device_id_type=MESH)

    greet(partner)
    greet(device(3, core))
    pl.when(x < 3)(lambda: greet(device(1, core)))
    pl.when(x == 3)(lambda: greet(device(-3, core)))
    pl.when(x == 0)(lambda: greet(device(4, core)))

    load = pltpu.make_async_copy(emb, raw, raw_sem)
    load.start()

    for half in range(2):
        part = offs[0:1, half * LANES:(half + 1) * LANES].astype(jnp.float32)
        table[half * LANES:(half + 1) * LANES, :] = jnp.broadcast_to(part, (LANES, LANES)).T

    def lane_ids(owner, group):
        first = (owner % DEVICES) * ROWS + group * LANES
        index = first + lax.broadcasted_iota(jnp.int32, (1, LANES), 1)
        hit = table[...] <= index.astype(jnp.float32)
        return jnp.sum(jnp.where(hit, 1.0, 0.0), axis=0, keepdims=True)

    extra_owner = jnp.where(core == 0, me + 1, me + 5)

    def fill_ids(group, _):
        rows = pl.ds(pl.multiple_of(group * LANES, LANES), LANES)
        mine = lane_ids(me, group)
        lane_own[group] = mine
        id_own[rows, :] = jnp.broadcast_to(mine, (LANES, LANES)).T
        away = lane_ids(me + 6, group)
        id_far[rows, :] = jnp.broadcast_to(away, (LANES, LANES)).T
        lane_far[group, :, 0:LANES] = away
        lane_far[group, :, LANES:2 * LANES] = lane_ids(extra_owner, group)
        lane_near[group, :, 0:LANES] = lane_ids(me + 2, group)
        lane_near[group, :, LANES:2 * LANES] = lane_ids(me + 3 - 2 * core, group)
        return 0

    lax.fori_loop(0, STEPS, fill_ids, 0)
    row_own[...] = jnp.full_like(row_own, -1.0)
    row_far[...] = jnp.full_like(row_far, -1.0)
    col_near[...] = jnp.full_like(col_near, -1.0)
    col_far[...] = jnp.full_like(col_far, -1.0)

    load.wait()

    def normalize(step, _):
        rows = pl.ds(pl.multiple_of(step * CHUNK, CHUNK), CHUNK)
        wide = raw[rows, :].astype(jnp.float32)
        mean = jnp.sum(wide * wide, axis=1, keepdims=True) * (1.0 / WIDTH)
        factor = lax.rsqrt(mean + 1e-06) * (1.0 / 32.0)
        own[rows, :] = (wide * factor).astype(jnp.bfloat16)
        return 0

    lax.fori_loop(0, STEPS, normalize, 0)

    @pl.when(x == 0)
    def _():
        pl.semaphore_wait(barrier, 4)

    @pl.when(x != 0)
    def _():
        pl.semaphore_wait(barrier, 3)

    def chunk(step):
        return own.at[pl.ds(pl.multiple_of(step * CHUNK, CHUNK), CHUNK)]

    def piece(step, part):
        return pl.ds(pl.multiple_of(step * CHUNK + part * PIECE, PIECE), PIECE)

    def near_copy(step):
        return remote(
            chunk(step), near.at[step, 0:CHUNK], near_s.at[step], near_r.at[step], device(-1, core)
        )

    def hop_copy(step, part):
        return remote(
            own.at[piece(step, part)], relay.at[piece(step, part)],
            near_s.at[step], relay_r.at[step, part], device(-4, core),
        )

    def pass_copy(step, part):
        return remote(
            relay.at[piece(step, part)], near.at[step, part * PIECE:(part + 1) * PIECE],
            hop_s.at[step], near_r.at[step], device(3, core),
        )

    def far_copy(step):
        return remote(
            chunk(step), far.at[step, 0:CHUNK], far_s.at[step], far_r.at[step], device(-3, core)
        )

    def swap_copy(step):
        return remote(
            near.at[step, 0:CHUNK], near.at[step, CHUNK:2 * CHUNK],
            swap_s.at[step], swap_r.at[step], partner,
        )

    def extra_own(step):
        return remote(
            chunk(step), far.at[step, CHUNK:2 * CHUNK], extra_s.at[step], extra_r.at[step], partner
        )

    def extra_far(step):
        return remote(
            far.at[step, 0:CHUNK], far.at[step, CHUNK:2 * CHUNK],
            extra_s.at[step], extra_r.at[step], partner,
        )

    def send(step, _):
        @pl.when(x != 0)
        def _():
            near_copy(step).start()

        @pl.when(x == 0)
        def _():
            for part in range(PIECES):
                hop_copy(step, part).start()

        far_copy(step).start()
        pl.when(core == 1)(lambda: extra_own(step).start())
        return 0

    lax.fori_loop(0, STEPS, send, 0)

    def fold(scores, ids, lanes, carried, column, other=None):
        width = scores.shape[1] // LANES
        for j in range(width):
            part = scores[:, j * LANES:(j + 1) * LANES]
            same = ids == lanes[:, j * LANES:(j + 1) * LANES]
            if other is not None:
                same = same & other[j]
            part = jnp.where(same, part, -1.0)
            carried = jnp.maximum(carried, part)
            if column is not None:
                column(j, jnp.max(part.reshape(part.shape[0] // 8, 8, LANES), axis=0))
        return carried

    def raise_to(ref, index):
        def update(j, value):
            at = (index, slice(None), slice(j * LANES, (j + 1) * LANES))
            ref[at] = jnp.maximum(ref[at], value)
        return update

    def diagonal(block, _):
        columns = pl.ds(pl.multiple_of(block * 2 * LANES, 2 * LANES), 2 * LANES)
        scores = dot(own[...], own[columns, :])
        rows = lax.broadcasted_iota(jnp.int32, (ROWS, LANES), 0)
        lanes = lax.broadcasted_iota(jnp.int32, (ROWS, LANES), 1) + block * 2 * LANES
        best = row_own[...]
        for j in range(2):
            part = scores[:, j * LANES:(j + 1) * LANES]
            same = (id_own[...] == lane_own[block * 2 + j]) & (rows != lanes + j * LANES)
            best = jnp.maximum(best, jnp.where(same, part, -1.0))
        row_own[...] = best
        return 0

    lax.fori_loop(0, ROWS // (2 * LANES), diagonal, 0)

    def far_block(first, count, step):
        left = far[pl.ds(first, count), 0:CHUNK, :].reshape(count * CHUNK, WIDTH)
        rows = pl.ds(pl.multiple_of(first * CHUNK, CHUNK), count * CHUNK)
        scores = dot(left, near[step])
        row_far[rows, :] = fold(
            scores, id_far[rows, :], lane_near[step], row_far[rows, :], raise_to(col_near, step)
        )

    def advance(step, _):
        @pl.when(x == 0)
        def _():
            for part in range(PIECES):
                hop_copy(step, part).wait_recv()
                pass_copy(step, part).start()

        near_copy(step).wait_recv()
        swap_copy(step).start()
        far_copy(step).wait_recv()
        pl.when(core == 0)(lambda: extra_far(step).start())
        extra_own(step).wait_recv()
        scores = dot(own[...], far[step])
        row_own[...] = fold(scores, id_own[...], lane_far[step], row_own[...], raise_to(col_far, step))
        swap_copy(step).wait_recv()
        scores = dot(own[...], near[step])
        row_own[...] = fold(scores, id_own[...], lane_near[step], row_own[...], raise_to(col_near, step))

        @pl.when((step % 2 == 1) & (step < STEPS - 1))
        def _():
            def fresh(other, _):
                far_block(step - 1, 2, other)
                return 0

            lax.fori_loop(0, step + 1, fresh, 0)

            def older(pair, _):
                far_block((pair // 2) * 2, 2, step - 1 + pair % 2)
                return 0

            lax.fori_loop(0, step - 1, older, 0)

        @pl.when(step == STEPS - 2)
        def _():
            far_block(0, STEPS - 2, step)

        return 0

    lax.fori_loop(0, STEPS, advance, 0)
    far_block(0, STEPS, STEPS - 1)

    def last(other, _):
        far_block(STEPS - 2, 2, other)
        return 0

    lax.fori_loop(0, STEPS - 1, last, 0)

    def flat(ref):
        return jnp.concatenate(
            [
                jnp.max(ref[g * LANES:(g + 1) * LANES, :].T, axis=0, keepdims=True)
                for g in range(STEPS)
            ],
            axis=0,
        )

    best_near = jnp.max(col_near[...], axis=1)
    best_far = jnp.max(col_far[...], axis=1)
    reply[0] = best_near[:, 0:LANES]
    reply[1] = best_near[:, LANES:2 * LANES]
    reply[2] = jnp.maximum(best_far[:, 0:LANES], flat(row_far))
    reply[3] = best_far[:, LANES:2 * LANES]

    def answer(slot, target):
        return remote(reply.at[slot], heard.at[slot], reply_s.at[slot], reply_r.at[slot], target)

    answer(2, device(3, core)).start()
    pl.when(core == 0)(lambda: answer(3, partner).start())
    pl.when(core == 1)(lambda: answer(3, device(3, 0)).start())
    answer(0, device(1, core)).start()
    answer(1, device(1, 1 - core)).start()
    best = flat(row_own)
    for slot in range(4):
        answer(slot, partner).wait_recv()
        best = jnp.maximum(best, heard[slot])
    out[...] = best

    def drain(step, _):
        near_copy(step).wait_send()
        far_copy(step).wait_send()
        swap_copy(step).wait_send()
        extra_own(step).wait_send()

        @pl.when(x == 0)
        def _():
            remote(
                chunk(step), near.at[step, 0:CHUNK], hop_s.at[step], near_r.at[step], partner
            ).wait_send()

        return 0

    lax.fori_loop(0, STEPS, drain, 0)
    for slot in range(4):
        answer(slot, partner).wait_send()


def shards(embeddings, offsets):
    block = pltpu.VMEM((ROWS, WIDTH), jnp.bfloat16)
    wide = pltpu.VMEM((ROWS, LANES), jnp.float32)
    steps = pltpu.SemaphoreType.DMA((STEPS,))
    best = pl.pallas_call(
        kernel,
        out_shape=jax.ShapeDtypeStruct((STEPS, LANES), jnp.float32),
        in_specs=[
            pl.BlockSpec(memory_space=pl.ANY),
            pl.BlockSpec(memory_space=pltpu.VMEM),
        ],
        out_specs=pl.BlockSpec(memory_space=pltpu.VMEM),
        scratch_shapes=[
            block, block, block,
            pltpu.VMEM((STEPS, 2 * CHUNK, WIDTH), jnp.bfloat16),
            pltpu.VMEM((STEPS, 2 * CHUNK, WIDTH), jnp.bfloat16),
            wide, wide,
            pltpu.VMEM((STEPS, 1, LANES), jnp.float32),
            pltpu.VMEM((STEPS, 1, 2 * LANES), jnp.float32),
            pltpu.VMEM((STEPS, 1, 2 * LANES), jnp.float32),
            pltpu.VMEM((2 * LANES, LANES), jnp.float32),
            wide, wide,
            pltpu.VMEM((STEPS, 8, 2 * LANES), jnp.float32),
            pltpu.VMEM((STEPS, 8, 2 * LANES), jnp.float32),
            pltpu.VMEM((4, STEPS, LANES), jnp.float32),
            pltpu.VMEM((4, STEPS, LANES), jnp.float32),
            pltpu.SemaphoreType.DMA(()),
            steps, steps, steps, steps, steps, pltpu.SemaphoreType.DMA((4,)),
            pltpu.SemaphoreType.DMA((STEPS, PIECES)),
            steps, steps, steps, steps, pltpu.SemaphoreType.DMA((4,)),
        ],
        compiler_params=pltpu.CompilerParams(
            collective_id=0, has_side_effects=True, vmem_limit_bytes=62 * 1024 * 1024
        ),
        name="match",
    )(embeddings, offsets.reshape(1, -1))
    return best.reshape(-1)


def solution(mesh):
    return jax.shard_map(
        shards,
        mesh=mesh,
        in_specs=(P(AXES, None), P()),
        out_specs=P(AXES),
        check_vma=False,
    )
```

time: 277 us -> 83.2 us (0.30)
  the two profiles are of different devices: /device:TPU:64 before, /device:TPU:1 now
where the time goes in v2:
time: 83.2 us; the launch traced here: 83 us
  Pallas kernels  80.5 us (97%)
  local copies, waits for them, and re-layouts  2.52 us (3%)
    pallas_call x1, Pallas kernels, shards(): pl.pallas_call(kernel, out_shape=jax.ShapeDtypeStruct((STEPS, LANES), jnp...  80.5 us

profile of v2, /device:TPU:1, one launch (start us, length us, event | category | flops | bytes accessed | tf_op | source)
XLA Modules:
  0.0 83.0 jit_solution(1371112857602250365)
XLA Ops:
  0.0 1.2 %reshape.6.offs = s32[1,257]{1,0:T(1,128)} reshape(s32[257]{0:T(512)} %param.3) | data formatting | bytes 2056 | tf_op jit(solution)/shard_map/reshape | solution.py:353
  1.2 80.5 %match.1 = f32[8,128]{1,0:T(8,128)} custom-call(bf16[1024,1024]{1,0:T(8,128)(2,1)} %emb.1, s32[1,257]{1,0:T(1,128)} %reshape.6.offs), custom_call_target="tpu_custom_call" | custom-call | tf_op jit(solution)/shard_map/match/pallas_call | solution.py:322
  81.8 1.3 %copy.4 = f32[1024]{0:T(1024)} copy(f32[1024]{0:T(1024)} %bitcast.1) | data formatting | bytes 8192

commit v3 on v2

v3 whole, which is shorter than its diff:
```python
import functools

import jax
import jax.numpy as jnp
from jax import lax
from jax.experimental import pallas as pl
from jax.experimental.pallas import tpu as pltpu
from jax.sharding import PartitionSpec as P

AXES = ("grp", "work")
MESH = pl.DeviceIdType.MESH
ROWS = 1024
WIDTH = 1024
STEPS = 8
CHUNK = ROWS // STEPS
PIECES = 4
PIECE = CHUNK // PIECES
CHIPS = 64
DEVICES = 2 * CHIPS
LANES = 128


def dot(left, right):
    return lax.dot_general(
        left, right, (((1,), (1,)), ((), ())), preferred_element_type=jnp.float32
    )


def kernel(
    emb, offs, out,
    raw, own, relay, gathered,
    id_own, id_rows, lane_own, lane_ids, table, row_own, columns, reply, heard,
    raw_sem, near_s, far_s, hop_s, swap_s, extra_s, reply_s,
    relay_r, near_r, swap_r, far_r, extra_r, reply_r,
):
    grp = lax.axis_index("grp")
    work = lax.axis_index("work")
    core = work % 2
    x = (work // 2) % 4
    chip = grp * 16 + work // 2
    me = chip * 2 + core

    def device(distance, which):
        target = (chip + distance + CHIPS) % CHIPS
        return (target // 16, (target % 16) * 2 + which)

    partner = device(0, 1 - core)

    def remote(src, dst, send, recv, target):
        return pltpu.make_async_remote_copy(
            src_ref=src, dst_ref=dst, send_sem=send, recv_sem=recv,
            device_id=target, device_id_type=MESH,
        )

    barrier = pltpu.get_barrier_semaphore()

    def greet(target):
        pl.semaphore_signal(barrier, inc=1, device_id=target, device_id_type=MESH)

    greet(device(3, core))
    pl.when(x == 0)(lambda: greet(device(4, core)))
    pl.when(x < 3)(lambda: greet(device(1, core)))
    pl.when(x == 3)(lambda: greet(device(-3, core)))
    greet(partner)

    def chunk_rows(step):
        return pl.ds(pl.multiple_of(step * CHUNK, CHUNK), CHUNK)

    def chunk(step):
        return own.at[chunk_rows(step)]

    def load(step):
        return pltpu.make_async_copy(
            emb.at[chunk_rows(step)], raw.at[chunk_rows(step)], raw_sem.at[step]
        )

    for step in range(STEPS):
        load(step).start()

    def normalize(step):
        load(step).wait()
        rows = chunk_rows(step)
        wide = raw[rows, :].astype(jnp.float32)
        mean = jnp.sum(wide * wide, axis=1, keepdims=True) * (1.0 / WIDTH)
        factor = lax.rsqrt(mean + 1e-06) * (1.0 / 32.0)
        own[rows, :] = (wide * factor).astype(jnp.bfloat16)

    def piece(step, part):
        return pl.ds(pl.multiple_of(step * CHUNK + part * PIECE, PIECE), PIECE)

    def slot(step, kind):
        return gathered.at[step, kind * CHUNK:(kind + 1) * CHUNK]

    def near_copy(step):
        return remote(
            chunk(step), slot(step, 0), near_s.at[step], near_r.at[step], device(-1, core)
        )

    def hop_copy(step, part):
        return remote(
            own.at[piece(step, part)], relay.at[piece(step, part)],
            near_s.at[step], relay_r.at[step, part], device(-4, core),
        )

    def pass_copy(step, part):
        return remote(
            relay.at[piece(step, part)], gathered.at[step, part * PIECE:(part + 1) * PIECE],
            hop_s.at[step], near_r.at[step], device(3, core),
        )

    def far_copy(step):
        return remote(
            chunk(step), slot(step, 2), far_s.at[step], far_r.at[step], device(-3, core)
        )

    def swap_copy(step):
        return remote(slot(step, 0), slot(step, 1), swap_s.at[step], swap_r.at[step], partner)

    def extra_own(step):
        return remote(chunk(step), slot(step, 3), extra_s.at[step], extra_r.at[step], partner)

    def extra_far(step):
        return remote(slot(step, 2), slot(step, 3), extra_s.at[step], extra_r.at[step], partner)

    def send(step):
        far_copy(step).start()

        @pl.when(x != 0)
        def _():
            near_copy(step).start()

        @pl.when(x == 0)
        def _():
            for part in range(PIECES):
                hop_copy(step, part).start()

        pl.when(core == 1)(lambda: extra_own(step).start())

    normalize(0)
    normalize(1)

    @pl.when(x == 0)
    def _():
        pl.semaphore_wait(barrier, 4)

    @pl.when(x != 0)
    def _():
        pl.semaphore_wait(barrier, 3)

    send(0)

    def start(step, _):
        normalize(step)
        send(step - 1)
        return 0

    lax.fori_loop(2, STEPS, start, 0)

    def fill_table(index, _):
        table[pl.ds(index, 1), :] = jnp.full((1, LANES), offs[index], jnp.int32)
        return 0

    lax.fori_loop(0, 2 * LANES, fill_table, 0, unroll=8)
    send(STEPS - 1)

    def ids_of(owner, group):
        first = (owner % DEVICES) * ROWS + group * LANES
        index = first + lax.broadcasted_iota(jnp.int32, (1, LANES), 1)
        return jnp.sum(jnp.where(table[...] <= index, 1.0, 0.0), axis=0, keepdims=True)

    extra_owner = jnp.where(core == 0, me + 1, me + 5)

    def fill_ids(group, _):
        mine = ids_of(me, group)
        lane_own[group] = mine
        id_own[chunk_rows(group), :] = jnp.broadcast_to(mine, (LANES, LANES)).T
        owners = (me + 2, me + 3 - 2 * core, me + 6, extra_owner)
        for kind in range(4):
            ids = ids_of(owners[kind], group)
            lane_ids[group, :, kind * LANES:(kind + 1) * LANES] = ids
            if kind < 3:
                id_rows[group, kind * LANES:(kind + 1) * LANES, :] = jnp.broadcast_to(
                    ids, (LANES, LANES)
                ).T
        return 0

    lax.fori_loop(0, STEPS, fill_ids, 0)
    row_own[...] = jnp.full_like(row_own, -1.0)
    columns[...] = jnp.full_like(columns, -1.0)

    def fold(scores, ids, lanes, carried, targets):
        for j in range(len(lanes)):
            part = scores[:, j * LANES:(j + 1) * LANES]
            part = jnp.where(ids == lanes[j], part, -1.0)
            carried = part if carried is None else jnp.maximum(carried, part)
            step, kind = targets[j]
            at = (step, slice(None), slice(kind * LANES, (kind + 1) * LANES))
            best = jnp.max(part.reshape(part.shape[0] // 8, 8, LANES), axis=0)
            columns[at] = jnp.maximum(columns[at], best)
        return carried

    def lanes_of(step, kind):
        return lane_ids[step, :, kind * LANES:(kind + 1) * LANES]

    def turned(rows):
        return jnp.max(rows.T, axis=0, keepdims=True)

    def diagonal(block, _):
        first = pl.multiple_of(block * 2 * LANES, 2 * LANES)
        scores = dot(own[...], own[pl.ds(first, 2 * LANES), :])
        rows = lax.broadcasted_iota(jnp.int32, (ROWS, LANES), 0)
        lanes = lax.broadcasted_iota(jnp.int32, (ROWS, LANES), 1) + first
        best = row_own[...]
        for j in range(2):
            part = scores[:, j * LANES:(j + 1) * LANES]
            same = (id_own[...] == lane_own[block * 2 + j]) & (rows != lanes + j * LANES)
            best = jnp.maximum(best, jnp.where(same, part, -1.0))
        row_own[...] = best
        return 0

    lax.fori_loop(0, ROWS // (2 * LANES), diagonal, 0)

    def older(step):
        right = gathered[0:step, 0:2 * CHUNK, :].reshape(step * 2 * CHUNK, WIDTH)
        scores = dot(gathered[step, 2 * CHUNK:3 * CHUNK, :], right)
        pairs = [(s, kind) for s in range(step) for kind in range(2)]
        best = fold(
            scores, id_rows[step, 2 * CHUNK:3 * CHUNK, :],
            [lanes_of(s, kind) for s, kind in pairs], None, pairs,
        )
        at = (step, slice(0, 1), slice(2 * LANES, 3 * LANES))
        columns[at] = jnp.maximum(columns[at], turned(best))

    def newer(step):
        right = gathered[0:step + 1, 2 * CHUNK:3 * CHUNK, :].reshape((step + 1) * CHUNK, WIDTH)
        scores = dot(gathered[step, 0:2 * CHUNK, :], right)
        pairs = [(s, 2) for s in range(step + 1)]
        best = fold(
            scores, id_rows[step, 0:2 * CHUNK, :],
            [lanes_of(s, kind) for s, kind in pairs], None, pairs,
        )
        for kind in range(2):
            at = (step, slice(0, 1), slice(kind * LANES, (kind + 1) * LANES))
            columns[at] = jnp.maximum(
                columns[at], turned(best[kind * LANES:(kind + 1) * LANES, :])
            )

    def advance(step, _):
        far_copy(step).wait_recv()
        pl.when(core == 0)(lambda: extra_far(step).start())

        @pl.when(x == 0)
        def _():
            for part in range(PIECES):
                hop_copy(step, part).wait_recv()
                pass_copy(step, part).start()

        near_copy(step).wait_recv()
        swap_copy(step).start()
        for known in range(1, STEPS):
            pl.when(step == known)(functools.partial(older, known))
        extra_own(step).wait_recv()
        swap_copy(step).wait_recv()
        scores = dot(own[...], gathered[step])
        row_own[...] = fold(
            scores, id_own[...], [lanes_of(step, kind) for kind in range(4)], row_own[...],
            [(step, kind) for kind in range(4)],
        )
        for known in range(STEPS):
            pl.when(step == known)(functools.partial(newer, known))
        return 0

    lax.fori_loop(0, STEPS, advance, 0)

    best = jnp.max(columns[...], axis=1)
    for kind in range(4):
        reply[kind] = best[:, kind * LANES:(kind + 1) * LANES]

    def answer(kind, target):
        return remote(
            reply.at[kind], heard.at[kind], reply_s.at[kind], reply_r.at[kind], target
        )

    answer(2, device(3, core)).start()
    answer(0, device(1, core)).start()
    answer(1, device(1, 1 - core)).start()
    pl.when(core == 0)(lambda: answer(3, partner).start())
    pl.when(core == 1)(lambda: answer(3, device(3, 0)).start())
    best = jnp.concatenate([turned(row_own[chunk_rows(g), :]) for g in range(STEPS)], axis=0)
    for kind in range(4):
        answer(kind, partner).wait_recv()
        best = jnp.maximum(best, heard[kind])
    out[...] = best

    def drain(step, _):
        near_copy(step).wait_send()
        far_copy(step).wait_send()
        swap_copy(step).wait_send()
        extra_own(step).wait_send()

        @pl.when(x == 0)
        def _():
            remote(
                chunk(step), slot(step, 0), hop_s.at[step], near_r.at[step], partner
            ).wait_send()

        return 0

    lax.fori_loop(0, STEPS, drain, 0)
    for kind in range(4):
        answer(kind, partner).wait_send()


def shards(embeddings, offsets):
    block = pltpu.VMEM((ROWS, WIDTH), jnp.bfloat16)
    wide = pltpu.VMEM((ROWS, LANES), jnp.float32)
    steps = pltpu.SemaphoreType.DMA((STEPS,))
    best = pl.pallas_call(
        kernel,
        out_shape=jax.ShapeDtypeStruct((STEPS, LANES), jnp.float32),
        in_specs=[
            pl.BlockSpec(memory_space=pl.ANY),
            pl.BlockSpec(memory_space=pltpu.SMEM),
        ],
        out_specs=pl.BlockSpec(memory_space=pltpu.VMEM),
        scratch_shapes=[
            block, block, block,
            pltpu.VMEM((STEPS, 4 * CHUNK, WIDTH), jnp.bfloat16),
            wide,
            pltpu.VMEM((STEPS, 3 * LANES, LANES), jnp.float32),
            pltpu.VMEM((STEPS, 1, LANES), jnp.float32),
            pltpu.VMEM((STEPS, 1, 4 * LANES), jnp.float32),
            pltpu.VMEM((2 * LANES, LANES), jnp.int32),
            wide,
            pltpu.VMEM((STEPS, 8, 4 * LANES), jnp.float32),
            pltpu.VMEM((4, STEPS, LANES), jnp.float32),
            pltpu.VMEM((4, STEPS, LANES), jnp.float32),
            steps,
            steps, steps, steps, steps, steps, pltpu.SemaphoreType.DMA((4,)),
            pltpu.SemaphoreType.DMA((STEPS, PIECES)),
            steps, steps, steps, steps, pltpu.SemaphoreType.DMA((4,)),
        ],
        compiler_params=pltpu.CompilerParams(
            collective_id=0, has_side_effects=True, vmem_limit_bytes=62 * 1024 * 1024
        ),
        name="match",
    )(embeddings, offsets)
    return best.reshape(-1)


def solution(mesh):
    return jax.shard_map(
        shards,
        mesh=mesh,
        in_specs=(P(AXES, None), P()),
        out_specs=P(AXES),
        check_vma=False,
    )
```

time: 83.2 us -> 76.7 us (0.922)
  Pallas kernels: 80.5 us -> 75.3 us
  local copies, waits for them, and re-layouts: 2.52 us -> 1.28 us
    pallas_call x1, Pallas kernels: 80.5 us -> 75.3 us  [shards(): pl.pallas_call(kernel, out_shape=jax.ShapeDtypeStruct((STEPS, LANES), jnp...]
    reshape x1 -> x0, local copies, waits for them, and re-layouts: 1.24 us -> none  [shards(): offsets.reshape(1, -1)]
where the time goes in v3:
time: 76.7 us; the launch traced here: 76.5 us
  Pallas kernels  75.3 us (98%)
  local copies, waits for them, and re-layouts  1.28 us (2%)
    pallas_call x1, Pallas kernels, shards(): pl.pallas_call(kernel, out_shape=jax.ShapeDtypeStruct((STEPS, LANES), jnp...  75.3 us

profile of v3, /device:TPU:1, one launch (start us, length us, event | category | flops | bytes accessed | tf_op | source)
XLA Modules:
  0.0 76.5 jit_solution(10253129171389110693)
XLA Ops:
  0.0 75.3 %match.1 = f32[8,128]{1,0:T(8,128)} custom-call(bf16[1024,1024]{1,0:T(8,128)(2,1)} %emb.1, s32[257]{0:T(512)} %offs.1), custom_call_target="tpu_custom_call" | custom-call | tf_op jit(solution)/shard_map/match/pallas_call | solution.py:318
  75.3 1.3 %copy.4 = f32[1024]{0:T(1024)} copy(f32[1024]{0:T(1024)} %bitcast.1) | data formatting | bytes 8192

commit v4 on v3

--- a/solution.py
+++ b/solution.py
@@ -13,8 +13,6 @@
 WIDTH = 1024
 STEPS = 8
 CHUNK = ROWS // STEPS
-PIECES = 4
-PIECE = CHUNK // PIECES
 CHIPS = 64
 DEVICES = 2 * CHIPS
 LANES = 128
@@ -28,10 +26,10 @@
 
 def kernel(
     emb, offs, out,
-    raw, own, relay, gathered,
-    id_own, id_rows, lane_own, lane_ids, table, row_own, columns, reply, heard,
-    raw_sem, near_s, far_s, hop_s, swap_s, extra_s, reply_s,
-    relay_r, near_r, swap_r, far_r, extra_r, reply_r,
+    raw, own, moved, gathered,
+    id_own, id_base, id_rows, lane_own, lane_ids, table, row_own, row_base, columns, reply, heard,
+    raw_sem, near_s, far_s, base_s, swap_s, extra_s, reply_s,
+    near_r, far_r, base_r, swap_r, extra_r, reply_r,
 ):
     grp = lax.axis_index("grp")
     work = lax.axis_index("work")
@@ -46,6 +44,14 @@
 
     partner = device(0, 1 - core)
 
+    last = x == 3
+    to_base = jnp.where(last, -4, 0)
+    to_near = to_base + 1
+    to_far = to_base + 3
+    near_host = device(jnp.where(x == 0, 3, -1), core)
+    far_host = device(jnp.where(x == 2, 1, -3), core)
+    base_host = device(4, core)
+
     def remote(src, dst, send, recv, target):
         return pltpu.make_async_remote_copy(
             src_ref=src, dst_ref=dst, send_sem=send, recv_sem=recv,
@@ -57,10 +63,9 @@
     def greet(target):
         pl.semaphore_signal(barrier, inc=1, device_id=target, device_id_type=MESH)
 
-    greet(device(3, core))
-    pl.when(x == 0)(lambda: greet(device(4, core)))
-    pl.when(x < 3)(lambda: greet(device(1, core)))
-    pl.when(x == 3)(lambda: greet(device(-3, core)))
+    greet(device(to_far, core))
+    greet(device(to_near, core))
+    pl.when(last)(lambda: greet(device(-4, core)))
     greet(partner)
 
     def chunk_rows(step):
@@ -85,33 +90,20 @@
         factor = lax.rsqrt(mean + 1e-06) * (1.0 / 32.0)
         own[rows, :] = (wide * factor).astype(jnp.bfloat16)
 
-    def piece(step, part):
-        return pl.ds(pl.multiple_of(step * CHUNK + part * PIECE, PIECE), PIECE)
-
     def slot(step, kind):
         return gathered.at[step, kind * CHUNK:(kind + 1) * CHUNK]
 
     def near_copy(step):
-        return remote(
-            chunk(step), slot(step, 0), near_s.at[step], near_r.at[step], device(-1, core)
-        )
-
-    def hop_copy(step, part):
-        return remote(
-            own.at[piece(step, part)], relay.at[piece(step, part)],
-            near_s.at[step], relay_r.at[step, part], device(-4, core),
-        )
-
-    def pass_copy(step, part):
-        return remote(
-            relay.at[piece(step, part)], gathered.at[step, part * PIECE:(part + 1) * PIECE],
-            hop_s.at[step], near_r.at[step], device(3, core),
-        )
+        return remote(chunk(step), slot(step, 0), near_s.at[step], near_r.at[step], near_host)
 
     def far_copy(step):
-        return remote(
-            chunk(step), slot(step, 2), far_s.at[step], far_r.at[step], device(-3, core)
-        )
+        return remote(chunk(step), slot(step, 2), far_s.at[step], far_r.at[step], far_host)
+
+    def base_chunk(step):
+        return moved.at[chunk_rows(step)]
+
+    def base_copy(step):
+        return remote(chunk(step), base_chunk(step), base_s.at[step], base_r.at[step], base_host)
 
     def swap_copy(step):
         return remote(slot(step, 0), slot(step, 1), swap_s.at[step], swap_r.at[step], partner)
@@ -122,28 +114,23 @@
     def extra_far(step):
         return remote(slot(step, 2), slot(step, 3), extra_s.at[step], extra_r.at[step], partner)
 
+    def extra_base(step):
+        return remote(base_chunk(step), slot(step, 3), extra_s.at[step], extra_r.at[step], partner)
+
     def send(step):
         far_copy(step).start()
-
-        @pl.when(x != 0)
-        def _():
-            near_copy(step).start()
-
-        @pl.when(x == 0)
-        def _():
-            for part in range(PIECES):
-                hop_copy(step, part).start()
-
-        pl.when(core == 1)(lambda: extra_own(step).start())
+        near_copy(step).start()
+        pl.when(last)(lambda: base_copy(step).start())
+        pl.when((core == 1) & (x < 3))(lambda: extra_own(step).start())
 
     normalize(0)
     normalize(1)
 
-    @pl.when(x == 0)
+    @pl.when(last)
     def _():
         pl.semaphore_wait(barrier, 4)
 
-    @pl.when(x != 0)
+    @pl.when(x < 3)
     def _():
         pl.semaphore_wait(barrier, 3)
 
@@ -168,13 +155,15 @@
         index = first + lax.broadcasted_iota(jnp.int32, (1, LANES), 1)
         return jnp.sum(jnp.where(table[...] <= index, 1.0, 0.0), axis=0, keepdims=True)
 
-    extra_owner = jnp.where(core == 0, me + 1, me + 5)
+    base = (me + 2 * to_base + DEVICES) % DEVICES
+    extra_owner = jnp.where(core == 0, base + 1, base + 5)
 
     def fill_ids(group, _):
         mine = ids_of(me, group)
         lane_own[group] = mine
         id_own[chunk_rows(group), :] = jnp.broadcast_to(mine, (LANES, LANES)).T
-        owners = (me + 2, me + 3 - 2 * core, me + 6, extra_owner)
+        id_base[chunk_rows(group), :] = jnp.broadcast_to(ids_of(base, group), (LANES, LANES)).T
+        owners = (base + 2, base + 3 - 2 * core, base + 6, extra_owner)
         for kind in range(4):
             ids = ids_of(owners[kind], group)
             lane_ids[group, :, kind * LANES:(kind + 1) * LANES] = ids
@@ -186,6 +175,7 @@
 
     lax.fori_loop(0, STEPS, fill_ids, 0)
     row_own[...] = jnp.full_like(row_own, -1.0)
+    row_base[...] = jnp.full_like(row_base, -1.0)
     columns[...] = jnp.full_like(columns, -1.0)
 
     def fold(scores, ids, lanes, carried, targets):
@@ -245,28 +235,52 @@
                 columns[at], turned(best[kind * LANES:(kind + 1) * LANES, :])
             )
 
+    kinds = range(4)
+
+    def base_older(step):
+        pairs = [(s, kind) for s in range(step) for kind in kinds]
+        rows = slice(step * CHUNK, (step + 1) * CHUNK)
+        scores = dot(moved[rows, :], gathered[0:step].reshape(step * 4 * CHUNK, WIDTH))
+        row_base[rows, :] = fold(
+            scores, id_base[rows, :], [lanes_of(s, kind) for s, kind in pairs],
+            row_base[rows, :], pairs,
+        )
+
+    def base_newer(step):
+        rows = slice(0, (step + 1) * CHUNK)
+        scores = dot(moved[rows, :], gathered[step])
+        row_base[rows, :] = fold(
+            scores, id_base[rows, :], [lanes_of(step, kind) for kind in kinds],
+            row_base[rows, :], [(step, kind) for kind in kinds],
+        )
+
     def advance(step, _):
         far_copy(step).wait_recv()
         pl.when(core == 0)(lambda: extra_far(step).start())
 
-        @pl.when(x == 0)
+        @pl.when(last)
         def _():
-            for part in range(PIECES):
-                hop_copy(step, part).wait_recv()
-                pass_copy(step, part).start()
+            base_copy(step).wait_recv()
+            pl.when(core == 1)(lambda: extra_base(step).start())
 
         near_copy(step).wait_recv()
         swap_copy(step).start()
         for known in range(1, STEPS):
             pl.when(step == known)(functools.partial(older, known))
+            pl.when((step == known) & last)(functools.partial(base_older, known))
         extra_own(step).wait_recv()
         swap_copy(step).wait_recv()
-        scores = dot(own[...], gathered[step])
-        row_own[...] = fold(
-            scores, id_own[...], [lanes_of(step, kind) for kind in range(4)], row_own[...],
-            [(step, kind) for kind in range(4)],
-        )
+
+        @pl.when(x < 3)
+        def _():
+            scores = dot(own[...], gathered[step])
+            row_base[...] = fold(
+                scores, id_base[...], [lanes_of(step, kind) for kind in kinds], row_base[...],
+                [(step, kind) for kind in kinds],
+            )
+
         for known in range(STEPS):
+            pl.when((step == known) & last)(functools.partial(base_newer, known))
             pl.when(step == known)(functools.partial(newer, known))
         return 0
 
@@ -281,16 +295,31 @@
             reply.at[kind], heard.at[kind], reply_s.at[kind], reply_r.at[kind], target
         )
 
-    answer(2, device(3, core)).start()
-    answer(0, device(1, core)).start()
-    answer(1, device(1, 1 - core)).start()
-    pl.when(core == 0)(lambda: answer(3, partner).start())
-    pl.when(core == 1)(lambda: answer(3, device(3, 0)).start())
-    best = jnp.concatenate([turned(row_own[chunk_rows(g), :]) for g in range(STEPS)], axis=0)
+    def flat(ref):
+        return jnp.concatenate([turned(ref[chunk_rows(g), :]) for g in range(STEPS)], axis=0)
+
+    answer(2, device(to_far, core)).start()
+    answer(0, device(to_near, core)).start()
+    answer(1, device(to_near, 1 - core)).start()
+    pl.when(core == 0)(lambda: answer(3, device(to_base, 1)).start())
+    pl.when(core == 1)(lambda: answer(3, device(to_far, 0)).start())
+    based = flat(row_base)
+    reply[4] = based
+    best = flat(row_own)
+
+    @pl.when(last)
+    def _():
+        answer(4, device(-4, core)).start()
+        answer(4, device(-4, core)).wait_recv()
+
+    @pl.when(x < 3)
+    def _():
+        heard[4] = based
+
     for kind in range(4):
         answer(kind, partner).wait_recv()
         best = jnp.maximum(best, heard[kind])
-    out[...] = best
+    out[...] = jnp.maximum(best, heard[4])
 
     def drain(step, _):
         near_copy(step).wait_send()
@@ -298,17 +327,13 @@
         swap_copy(step).wait_send()
         extra_own(step).wait_send()
 
-        @pl.when(x == 0)
-        def _():
-            remote(
-                chunk(step), slot(step, 0), hop_s.at[step], near_r.at[step], partner
-            ).wait_send()
-
+        pl.when(last)(lambda: base_copy(step).wait_send())
         return 0
 
     lax.fori_loop(0, STEPS, drain, 0)
     for kind in range(4):
         answer(kind, partner).wait_send()
+    pl.when(last)(lambda: answer(4, partner).wait_send())
 
 
 def shards(embeddings, offsets):
@@ -326,19 +351,18 @@
         scratch_shapes=[
             block, block, block,
             pltpu.VMEM((STEPS, 4 * CHUNK, WIDTH), jnp.bfloat16),
-            wide,
+            wide, wide,
             pltpu.VMEM((STEPS, 3 * LANES, LANES), jnp.float32),
             pltpu.VMEM((STEPS, 1, LANES), jnp.float32),
             pltpu.VMEM((STEPS, 1, 4 * LANES), jnp.float32),
             pltpu.VMEM((2 * LANES, LANES), jnp.int32),
-            wide,
+            wide, wide,
             pltpu.VMEM((STEPS, 8, 4 * LANES), jnp.float32),
-            pltpu.VMEM((4, STEPS, LANES), jnp.float32),
-            pltpu.VMEM((4, STEPS, LANES), jnp.float32),
+            pltpu.VMEM((5, STEPS, LANES), jnp.float32),
+            pltpu.VMEM((5, STEPS, LANES), jnp.float32),
             steps,
-            steps, steps, steps, steps, steps, pltpu.SemaphoreType.DMA((4,)),
-            pltpu.SemaphoreType.DMA((STEPS, PIECES)),
-            steps, steps, steps, steps, pltpu.SemaphoreType.DMA((4,)),
+            steps, steps, steps, steps, steps, pltpu.SemaphoreType.DMA((5,)),
+            steps, steps, steps, steps, steps, pltpu.SemaphoreType.DMA((5,)),
         ],
         compiler_params=pltpu.CompilerParams(
             collective_id=0, has_side_effects=True, vmem_limit_bytes=62 * 1024 * 1024

time: 76.7 us -> 69.6 us (0.907)
  Pallas kernels: 75.3 us -> 68.2 us
    pallas_call x1, Pallas kernels: 75.3 us -> 68.2 us  [shards(): pl.pallas_call(kernel, out_shape=jax.ShapeDtypeStruct((STEPS, LANES), jnp...]
where the time goes in v4:
time: 69.6 us; the launch traced here: 69.4 us
  Pallas kernels  68.2 us (98%)
  local copies, waits for them, and re-layouts  1.28 us (2%)
    pallas_call x1, Pallas kernels, shards(): pl.pallas_call(kernel, out_shape=jax.ShapeDtypeStruct((STEPS, LANES), jnp...  68.2 us

profile of v4, /device:TPU:1, one launch (start us, length us, event | category | flops | bytes accessed | tf_op | source)
XLA Modules:
  0.0 69.4 jit_solution(10554111318347653962)
XLA Ops:
  0.0 68.2 %match.1 = f32[8,128]{1,0:T(8,128)} custom-call(bf16[1024,1024]{1,0:T(8,128)(2,1)} %emb.1, s32[257]{0:T(512)} %offs.1), custom_call_target="tpu_custom_call" | custom-call | tf_op jit(solution)/shard_map/match/pallas_call | solution.py:343
  68.2 1.3 %copy.4 = f32[1024]{0:T(1024)} copy(f32[1024]{0:T(1024)} %bitcast.1) | data formatting | bytes 8192

commit v5 on v4

v5 whole, which is shorter than its diff:
```python
import functools

import jax
import jax.numpy as jnp
from jax import lax
from jax.experimental import pallas as pl
from jax.experimental.pallas import tpu as pltpu
from jax.sharding import PartitionSpec as P

AXES = ("grp", "work")
MESH = pl.DeviceIdType.MESH
ROWS = 1024
WIDTH = 1024
STEPS = 8
CHUNK = ROWS // STEPS
CHIPS = 64
BASE, FAR, NEAR, SWAP, EXTRA = range(5)
DEVICES = 2 * CHIPS
LANES = 128


def dot(left, right):
    return lax.dot_general(
        left, right, (((1,), (1,)), ((), ())), preferred_element_type=jnp.float32
    )


def kernel(
    emb, offs, out,
    raw, own, mate, gathered,
    id_own, id_rows, lane_own, lane_ids, table, row_own, row_base, columns, reply, heard, mate_best,
    raw_sem, near_s, far_s, base_s, swap_s, extra_s, reply_s,
    near_r, far_r, base_r, swap_r, extra_r, reply_r, mate_sems,
):
    grp = lax.axis_index("grp")
    work = lax.axis_index("work")
    core = work % 2
    x = (work // 2) % 4
    chip = grp * 16 + work // 2
    me = chip * 2 + core

    def device(distance, which):
        target = (chip + distance + CHIPS) % CHIPS
        return (target // 16, (target % 16) * 2 + which)

    partner = device(0, 1 - core)

    last = x == 3
    to_base = jnp.where(last, -4, 0)
    to_near = to_base + 1
    to_far = to_base + 3
    near_host = device(jnp.where(x == 0, 3, -1), core)
    far_host = device(jnp.where(x == 2, 1, -3), core)
    base_host = device(4, core)
    sends_far = chip >= 2
    sends_base = last & (chip != CHIPS - 1)
    has_far = (chip != CHIPS - 3) & (chip != CHIPS - 2)
    has_base = last & (chip != 3)
    has_extra = jnp.where(core == 1, has_far, chip != 3)
    sends_extra = jnp.where(core == 0, has_far, chip != 3)
    sends_back = has_extra

    def remote(src, dst, send, recv, target):
        return pltpu.make_async_remote_copy(
            src_ref=src, dst_ref=dst, send_sem=send, recv_sem=recv,
            device_id=target, device_id_type=MESH,
        )

    barrier = pltpu.get_barrier_semaphore()

    def greet(target):
        pl.semaphore_signal(barrier, inc=1, device_id=target, device_id_type=MESH)

    pl.when(has_far)(lambda: greet(device(to_far, core)))
    greet(device(to_near, core))
    pl.when(has_base)(lambda: greet(device(-4, core)))
    greet(partner)

    def chunk_rows(step):
        return pl.ds(pl.multiple_of(step * CHUNK, CHUNK), CHUNK)

    def chunk(step):
        return own.at[chunk_rows(step)]

    def load(step):
        return pltpu.make_async_copy(
            emb.at[chunk_rows(step)], raw.at[chunk_rows(step)], raw_sem.at[step]
        )

    for step in range(STEPS):
        load(step).start()

    def normalize(step):
        load(step).wait()
        rows = chunk_rows(step)
        wide = raw[rows, :].astype(jnp.float32)
        mean = jnp.sum(wide * wide, axis=1, keepdims=True) * (1.0 / WIDTH)
        factor = lax.rsqrt(mean + 1e-06) * (1.0 / 32.0)
        own[rows, :] = (wide * factor).astype(jnp.bfloat16)

    def slot(step, kind):
        return gathered.at[step, kind * CHUNK:(kind + 1) * CHUNK]

    def near_copy(step):
        return remote(chunk(step), slot(step, NEAR), near_s.at[step], near_r.at[step], near_host)

    def far_copy(step):
        return remote(chunk(step), slot(step, FAR), far_s.at[step], far_r.at[step], far_host)

    def base_copy(step):
        return remote(chunk(step), slot(step, BASE), base_s.at[step], base_r.at[step], base_host)

    def swap_copy(step):
        return remote(slot(step, NEAR), slot(step, SWAP), swap_s.at[step], swap_r.at[step], partner)

    def extra_own(step):
        return remote(chunk(step), slot(step, EXTRA), extra_s.at[step], extra_r.at[step], partner)

    def extra_far(step):
        return remote(slot(step, FAR), slot(step, EXTRA), extra_s.at[step], extra_r.at[step], partner)

    def extra_base(step):
        return remote(slot(step, BASE), slot(step, EXTRA), extra_s.at[step], extra_r.at[step], partner)

    def send(step):
        pl.when(sends_far)(lambda: far_copy(step).start())
        near_copy(step).start()
        pl.when(sends_base)(lambda: base_copy(step).start())
        pl.when((core == 1) & (x < 3))(lambda: extra_own(step).start())

    normalize(0)
    normalize(1)

    @pl.when(sends_base)
    def _():
        pl.semaphore_wait(barrier, 4)

    @pl.when(sends_far & jnp.logical_not(sends_base))
    def _():
        pl.semaphore_wait(barrier, 3)

    @pl.when(jnp.logical_not(sends_far))
    def _():
        pl.semaphore_wait(barrier, 2)

    send(0)

    def start(step, _):
        normalize(step)
        send(step - 1)
        return 0

    lax.fori_loop(2, STEPS, start, 0)

    def fill_table(index, _):
        table[pl.ds(index, 1), :] = jnp.full((1, LANES), offs[index], jnp.int32)
        return 0

    lax.fori_loop(0, 2 * LANES, fill_table, 0, unroll=8)
    send(STEPS - 1)

    alone = chip == CHIPS - 1

    def mate_copy():
        return remote(own, mate, mate_sems.at[0], mate_sems.at[1], partner)

    def mate_answer():
        return remote(
            mate_best, heard.at[EXTRA], mate_sems.at[2], reply_r.at[EXTRA], partner
        )

    pl.when(alone & (core == 1))(lambda: mate_copy().start())

    def ids_of(owner, group):
        first = (owner % DEVICES) * ROWS + group * LANES
        index = first + lax.broadcasted_iota(jnp.int32, (1, LANES), 1)
        return jnp.sum(jnp.where(table[...] <= index, 1.0, 0.0), axis=0, keepdims=True)

    base = (me + 2 * to_base + DEVICES) % DEVICES
    extra_owner = jnp.where(core == 0, base + 1, base + 5)

    def fill_ids(group, _):
        mine = ids_of(me, group)
        lane_own[group] = mine
        id_own[chunk_rows(group), :] = jnp.broadcast_to(mine, (LANES, LANES)).T
        owners = (base, base + 6, base + 2, base + 3 - 2 * core, extra_owner)
        for kind in range(5):
            ids = ids_of(owners[kind], group)
            if kind != BASE:
                lane_ids[group, :, (kind - 1) * LANES:kind * LANES] = ids
            if kind != EXTRA:
                id_rows[group, kind * LANES:(kind + 1) * LANES, :] = jnp.broadcast_to(
                    ids, (LANES, LANES)
                ).T
        return 0

    lax.fori_loop(0, STEPS, fill_ids, 0)
    row_own[...] = jnp.full_like(row_own, -1.0)
    row_base[...] = jnp.full_like(row_base, -1.0)
    columns[...] = jnp.full_like(columns, -1.0)

    def fill(kind):
        def one(step, _):
            gathered[step, kind * CHUNK:(kind + 1) * CHUNK, :] = own[chunk_rows(step), :]
            return 0
        lax.fori_loop(0, STEPS, one, 0)

    pl.when(jnp.logical_not(has_far))(lambda: fill(FAR))
    pl.when(last & jnp.logical_not(has_base))(lambda: fill(BASE))
    pl.when(jnp.logical_not(has_extra))(lambda: fill(EXTRA))

    def place(step, kind, rows=slice(None)):
        return (step, rows, slice((kind - 1) * LANES, kind * LANES))

    def raise_to(target, part):
        best = jnp.max(part.reshape(part.shape[0] // 8, 8, LANES), axis=0)
        columns[place(*target)] = jnp.maximum(columns[place(*target)], best)

    def fold(scores, ids, lanes, carried, targets):
        for j in range(len(lanes)):
            part = scores[:, j * LANES:(j + 1) * LANES]
            part = jnp.where(ids == lanes[j], part, -1.0)
            carried = part if carried is None else jnp.maximum(carried, part)
            raise_to(targets[j], part)
        return carried

    def lanes_of(step, kind):
        return lane_ids[step, :, (kind - 1) * LANES:kind * LANES]

    def turned(rows):
        return jnp.max(rows.T, axis=0, keepdims=True)

    def diagonal(block, _):
        first = pl.multiple_of(block * 2 * LANES, 2 * LANES)
        scores = dot(own[...], own[pl.ds(first, 2 * LANES), :])
        rows = lax.broadcasted_iota(jnp.int32, (ROWS, LANES), 0)
        lanes = lax.broadcasted_iota(jnp.int32, (ROWS, LANES), 1) + first
        best = row_own[...]
        for j in range(2):
            part = scores[:, j * LANES:(j + 1) * LANES]
            same = (id_own[...] == lane_own[block * 2 + j]) & (rows != lanes + j * LANES)
            best = jnp.maximum(best, jnp.where(same, part, -1.0))
        row_own[...] = best
        return 0

    lax.fori_loop(0, ROWS // (2 * LANES), diagonal, 0)

    @pl.when(alone & (core == 0))
    def _():
        mate_copy().wait_recv()

        def against(block, _):
            first = pl.multiple_of(block * 2 * LANES, 2 * LANES)
            scores = dot(own[...], mate[pl.ds(first, 2 * LANES), :])
            best = row_own[...]
            for j in range(2):
                same = id_own[...] == ids_of(me + 1, block * 2 + j)
                part = jnp.where(same, scores[:, j * LANES:(j + 1) * LANES], -1.0)
                best = jnp.maximum(best, part)
                mate_best[pl.ds(block * 2 + j, 1), :] = jnp.max(part, axis=0, keepdims=True)
            row_own[...] = best
            return 0

        lax.fori_loop(0, ROWS // (2 * LANES), against, 0)
        mate_answer().start()

    def settle(step, kind, rows):
        at = place(step, kind, slice(0, 1))
        columns[at] = jnp.maximum(columns[at], turned(rows))

    def older(step):
        right = gathered[0:step, NEAR * CHUNK:EXTRA * CHUNK, :].reshape(step * 2 * CHUNK, WIDTH)
        scores = dot(gathered[step, FAR * CHUNK:NEAR * CHUNK, :], right)
        pairs = [(s, kind) for s in range(step) for kind in (NEAR, SWAP)]
        best = fold(
            scores, id_rows[step, FAR * CHUNK:NEAR * CHUNK, :],
            [lanes_of(s, kind) for s, kind in pairs], None, pairs,
        )
        settle(step, FAR, best)

    def older_both(step):
        right = gathered[0:step, FAR * CHUNK:, :].reshape(step * 4 * CHUNK, WIDTH)
        scores = dot(gathered[step, 0:NEAR * CHUNK, :], right)
        base_ids = id_rows[step, 0:CHUNK, :]
        far_ids = id_rows[step, CHUNK:2 * CHUNK, :]
        rows = slice(step * CHUNK, (step + 1) * CHUNK)
        best_base, best_far = row_base[rows, :], jnp.full((CHUNK, LANES), -1.0, jnp.float32)
        for j, (s, kind) in enumerate((s, kind) for s in range(step) for kind in range(1, 5)):
            lanes = lanes_of(s, kind)
            part = jnp.where(base_ids == lanes, scores[0:CHUNK, j * LANES:(j + 1) * LANES], -1.0)
            best_base = jnp.maximum(best_base, part)
            if kind in (NEAR, SWAP):
                more = jnp.where(
                    far_ids == lanes, scores[CHUNK:, j * LANES:(j + 1) * LANES], -1.0
                )
                best_far = jnp.maximum(best_far, more)
                part = jnp.maximum(part, more)
            raise_to((s, kind), part)
        row_base[rows, :] = best_base
        settle(step, FAR, best_far)

    def newer(step):
        right = gathered[0:step + 1, FAR * CHUNK:NEAR * CHUNK, :].reshape((step + 1) * CHUNK, WIDTH)
        scores = dot(gathered[step, NEAR * CHUNK:EXTRA * CHUNK, :], right)
        pairs = [(s, FAR) for s in range(step + 1)]
        best = fold(
            scores, id_rows[step, NEAR * CHUNK:EXTRA * CHUNK, :],
            [lanes_of(s, kind) for s, kind in pairs], None, pairs,
        )
        settle(step, NEAR, best[0:CHUNK, :])
        settle(step, SWAP, best[CHUNK:, :])

    kinds = range(1, 5)

    def base_newer(step):
        count = (step + 1) * CHUNK
        left = gathered[0:step + 1, 0:CHUNK, :].reshape(count, WIDTH)
        ids = id_rows[0:step + 1, 0:CHUNK, :].reshape(count, LANES)
        row_base[0:count, :] = fold(
            dot(left, gathered[step, FAR * CHUNK:, :]), ids,
            [lanes_of(step, kind) for kind in kinds], row_base[0:count, :],
            [(step, kind) for kind in kinds],
        )

    def advance(step, _):
        @pl.when(has_far)
        def _():
            far_copy(step).wait_recv()
            pl.when(core == 0)(lambda: extra_far(step).start())

        @pl.when(has_base)
        def _():
            base_copy(step).wait_recv()
            pl.when(core == 1)(lambda: extra_base(step).start())

        near_copy(step).wait_recv()
        swap_copy(step).start()
        for known in range(1, STEPS):
            pl.when((step == known) & (x < 3))(functools.partial(older, known))
            pl.when((step == known) & last)(functools.partial(older_both, known))
        pl.when(has_extra)(lambda: extra_own(step).wait_recv())
        swap_copy(step).wait_recv()

        @pl.when(x < 3)
        def _():
            scores = dot(own[...], gathered[step, FAR * CHUNK:, :])
            row_base[...] = fold(
                scores, id_own[...], [lanes_of(step, kind) for kind in kinds], row_base[...],
                [(step, kind) for kind in kinds],
            )

        for known in range(STEPS):
            pl.when((step == known) & last)(functools.partial(base_newer, known))
            pl.when(step == known)(functools.partial(newer, known))
        return 0

    lax.fori_loop(0, STEPS, advance, 0)

    best = jnp.max(columns[...], axis=1)
    for kind in kinds:
        reply[kind] = best[:, (kind - 1) * LANES:kind * LANES]

    def answer(kind, target):
        return remote(
            reply.at[kind], heard.at[kind], reply_s.at[kind], reply_r.at[kind], target
        )

    def flat(ref):
        return jnp.concatenate([turned(ref[chunk_rows(g), :]) for g in range(STEPS)], axis=0)

    pl.when(has_far)(lambda: answer(FAR, device(to_far, core)).start())
    answer(NEAR, device(to_near, core)).start()
    answer(SWAP, device(to_near, 1 - core)).start()
    pl.when((core == 0) & sends_back)(lambda: answer(EXTRA, device(to_base, 1)).start())
    pl.when((core == 1) & sends_back)(lambda: answer(EXTRA, device(to_far, 0)).start())
    based = flat(row_base)
    reply[BASE] = based
    best = flat(row_own)
    pl.when(has_base)(lambda: answer(BASE, device(-4, core)).start())
    nothing = jnp.full((STEPS, LANES), -1.0, jnp.float32)

    def hear(kind, comes, instead):
        @pl.when(comes)
        def _():
            answer(kind, partner).wait_recv()

        @pl.when(jnp.logical_not(comes))
        def _():
            heard[kind] = instead

    hear(BASE, sends_base, jnp.where(last, nothing, based))
    hear(FAR, sends_far, nothing)
    hear(EXTRA, (core == 1) | sends_far, nothing)
    answer(NEAR, partner).wait_recv()
    answer(SWAP, partner).wait_recv()
    for kind in range(5):
        best = jnp.maximum(best, heard[kind])
    out[...] = best

    def drain(step, _):
        near_copy(step).wait_send()
        pl.when(sends_far)(lambda: far_copy(step).wait_send())
        swap_copy(step).wait_send()
        pl.when(sends_extra)(lambda: extra_own(step).wait_send())

        pl.when(sends_base)(lambda: base_copy(step).wait_send())
        return 0

    lax.fori_loop(0, STEPS, drain, 0)
    answer(NEAR, partner).wait_send()
    answer(SWAP, partner).wait_send()
    pl.when(has_far)(lambda: answer(FAR, partner).wait_send())
    pl.when(has_base)(lambda: answer(BASE, partner).wait_send())
    pl.when(sends_back)(lambda: answer(EXTRA, partner).wait_send())
    pl.when(alone & (core == 1))(lambda: mate_copy().wait_send())
    pl.when(alone & (core == 0))(lambda: mate_answer().wait_send())


def shards(embeddings, offsets):
    block = pltpu.VMEM((ROWS, WIDTH), jnp.bfloat16)
    wide = pltpu.VMEM((ROWS, LANES), jnp.float32)
    steps = pltpu.SemaphoreType.DMA((STEPS,))
    best = pl.pallas_call(
        kernel,
        out_shape=jax.ShapeDtypeStruct((STEPS, LANES), jnp.float32),
        in_specs=[
            pl.BlockSpec(memory_space=pl.ANY),
            pl.BlockSpec(memory_space=pltpu.SMEM),
        ],
        out_specs=pl.BlockSpec(memory_space=pltpu.VMEM),
        scratch_shapes=[
            block, block, block,
            pltpu.VMEM((STEPS, 5 * CHUNK, WIDTH), jnp.bfloat16),
            wide,
            pltpu.VMEM((STEPS, 4 * LANES, LANES), jnp.float32),
            pltpu.VMEM((STEPS, 1, LANES), jnp.float32),
            pltpu.VMEM((STEPS, 1, 4 * LANES), jnp.float32),
            pltpu.VMEM((2 * LANES, LANES), jnp.int32),
            wide, wide,
            pltpu.VMEM((STEPS, 8, 4 * LANES), jnp.float32),
            pltpu.VMEM((5, STEPS, LANES), jnp.float32),
            pltpu.VMEM((5, STEPS, LANES), jnp.float32),
            pltpu.VMEM((STEPS, LANES), jnp.float32),
            steps,
            steps, steps, steps, steps, steps, pltpu.SemaphoreType.DMA((5,)),
            steps, steps, steps, steps, steps, pltpu.SemaphoreType.DMA((5,)),
            pltpu.SemaphoreType.DMA((3,)),
        ],
        compiler_params=pltpu.CompilerParams(
            collective_id=0, has_side_effects=True, vmem_limit_bytes=62 * 1024 * 1024
        ),
        name="match",
    )(embeddings, offsets)
    return best.reshape(-1)


def solution(mesh):
    return jax.shard_map(
        shards,
        mesh=mesh,
        in_specs=(P(AXES, None), P()),
        out_specs=P(AXES),
        check_vma=False,
    )
```

time: 69.6 us -> 63.2 us (0.908); the launches traced: 69.4 us -> 62.1 us
  Pallas kernels: 68.2 us -> 60.8 us
    pallas_call x1, Pallas kernels: 68.2 us -> 60.8 us  [shards(): pl.pallas_call(kernel, out_shape=jax.ShapeDtypeStruct((STEPS, LANES), jnp...]
where the time goes in v5:
time: 63.2 us; the launch traced here: 62.1 us
  Pallas kernels  60.8 us (96%)
  local copies, waits for them, and re-layouts  1.28 us (2%)
    pallas_call x1, Pallas kernels, shards(): pl.pallas_call(kernel, out_shape=jax.ShapeDtypeStruct((STEPS, LANES), jnp...  60.8 us
    unnamed x1, local copies, waits for them, and re-layouts  1.28 us

profile of v5, /device:TPU:1, one launch (start us, length us, event | category | flops | bytes accessed | tf_op | source)
XLA Modules:
  0.0 62.1 jit_solution(3017870035074761236)
XLA Ops:
  0.0 60.8 %match.1 = f32[8,128]{1,0:T(8,128)} custom-call(bf16[1024,1024]{1,0:T(8,128)(2,1)} %emb.1, s32[257]{0:T(512)} %offs.1), custom_call_target="tpu_custom_call" | custom-call | tf_op jit(solution)/shard_map/match/pallas_call | solution.py:423
  60.8 1.3 %copy.4 = f32[1024]{0:T(1024)} copy(f32[1024]{0:T(1024)} %bitcast.1) | data formatting | bytes 8192

commit v6 on v5

--- a/solution.py
+++ b/solution.py
@@ -447,7 +447,7 @@
             pltpu.SemaphoreType.DMA((3,)),
         ],
         compiler_params=pltpu.CompilerParams(
-            collective_id=0, has_side_effects=True, vmem_limit_bytes=62 * 1024 * 1024
+            collective_id=0, has_side_effects=True, vmem_limit_bytes=53 * 1024 * 1024
         ),
         name="match",
     )(embeddings, offsets)

time: 63.2 us -> 62.5 us (0.989)
  Pallas kernels: 60.8 us -> 60.1 us
    pallas_call x1, Pallas kernels: 60.8 us -> 60.1 us  [shards(): pl.pallas_call(kernel, out_shape=jax.ShapeDtypeStruct((STEPS, LANES), jnp...]
    unnamed x1 -> x3, local copies, waits for them, and re-layouts: 1.28 us -> 1.28 us
where the time goes in v6:
time: 62.5 us; the launch traced here: 61.4 us
  Pallas kernels  60.1 us (96%)
  local copies, waits for them, and re-layouts  1.28 us (2%)
    pallas_call x1, Pallas kernels, shards(): pl.pallas_call(kernel, out_shape=jax.ShapeDtypeStruct((STEPS, LANES), jnp...  60.1 us
    unnamed x3, local copies, waits for them, and re-layouts  1.28 us

profile of v6, /device:TPU:1, one launch (start us, length us, event | category | flops | bytes accessed | tf_op | source)
XLA Modules:
  0.0 61.4 jit_solution(1816041861009954428)
XLA Ops:
  0.0 0.0 copy-start
  0.0 0.7 %copy-done = s32[257]{0:T(512)S(1)} copy-done((s32[257]{0:T(512)S(1)}, s32[257]{0:T(512)}, u32[]{:S(2)}) %copy-start) | copy-done | bytes 1052
  0.7 60.1 %match.1 = f32[8,128]{1,0:T(8,128)S(1)} custom-call(bf16[1024,1024]{1,0:T(8,128)(2,1)} %emb.1, s32[257]{0:T(512)S(1)} %copy-done), custom_call_target="tpu_custom_call" | custom-call | tf_op jit(solution)/shard_map/match/pallas_call | solution.py:423
  60.8 0.6 copy.4
Async XLA Ops:
  0.0 0.7 %copy-start = (s32[257]{0:T(512)S(1)}, s32[257]{0:T(512)}, u32[]{:S(2)}) copy-start(s32[257]{0:T(512)} %offs.1) | copy-start | bytes 3088

commit v7 on v6

--- a/solution.py
+++ b/solution.py
@@ -27,9 +27,9 @@
 
 def kernel(
     emb, offs, out,
-    raw, own, mate, gathered,
+    raw, own, mate, gathered, starts,
     id_own, id_rows, lane_own, lane_ids, table, row_own, row_base, columns, reply, heard, mate_best,
-    raw_sem, near_s, far_s, base_s, swap_s, extra_s, reply_s,
+    raw_sem, starts_sem, near_s, far_s, base_s, swap_s, extra_s, reply_s,
     near_r, far_r, base_r, swap_r, extra_r, reply_r, mate_sems,
 ):
     grp = lax.axis_index("grp")
@@ -89,6 +89,8 @@
 
     for step in range(STEPS):
         load(step).start()
+    load_starts = pltpu.make_async_copy(offs, starts, starts_sem)
+    load_starts.start()
 
     def normalize(step):
         load(step).wait()
@@ -153,9 +155,10 @@
     lax.fori_loop(2, STEPS, start, 0)
 
     def fill_table(index, _):
-        table[pl.ds(index, 1), :] = jnp.full((1, LANES), offs[index], jnp.int32)
-        return 0
-
+        table[pl.ds(index, 1), :] = jnp.full((1, LANES), starts[index], jnp.int32)
+        return 0
+
+    load_starts.wait()
     lax.fori_loop(0, 2 * LANES, fill_table, 0, unroll=8)
     send(STEPS - 1)
 
@@ -425,12 +428,13 @@
         out_shape=jax.ShapeDtypeStruct((STEPS, LANES), jnp.float32),
         in_specs=[
             pl.BlockSpec(memory_space=pl.ANY),
-            pl.BlockSpec(memory_space=pltpu.SMEM),
+            pl.BlockSpec(memory_space=pltpu.HBM),
         ],
         out_specs=pl.BlockSpec(memory_space=pltpu.VMEM),
         scratch_shapes=[
             block, block, block,
             pltpu.VMEM((STEPS, 5 * CHUNK, WIDTH), jnp.bfloat16),
+            pltpu.SMEM((257,), jnp.int32),
             wide,
             pltpu.VMEM((STEPS, 4 * LANES, LANES), jnp.float32),
             pltpu.VMEM((STEPS, 1, LANES), jnp.float32),
@@ -441,7 +445,7 @@
             pltpu.VMEM((5, STEPS, LANES), jnp.float32),
             pltpu.VMEM((5, STEPS, LANES), jnp.float32),
             pltpu.VMEM((STEPS, LANES), jnp.float32),
-            steps,
+            steps, pltpu.SemaphoreType.DMA(()),
             steps, steps, steps, steps, steps, pltpu.SemaphoreType.DMA((5,)),
             steps, steps, steps, steps, steps, pltpu.SemaphoreType.DMA((5,)),
             pltpu.SemaphoreType.DMA((3,)),
@@ -450,7 +454,7 @@
             collective_id=0, has_side_effects=True, vmem_limit_bytes=53 * 1024 * 1024
         ),
         name="match",
-    )(embeddings, offsets)
+    )(embeddings, pltpu.with_memory_space_constraint(offsets, pltpu.HBM))
     return best.reshape(-1)
 
 

time: 62.5 us -> 61.1 us (0.978)
  local copies, waits for them, and re-layouts: 1.28 us -> 0.6 us
    unnamed x3 -> x1, local copies, waits for them, and re-layouts: 1.28 us -> 0.6 us
    pallas_call x1, Pallas kernels: 60.1 us -> 59.5 us  [shards(): pl.pallas_call(kernel, out_shape=jax.ShapeDtypeStruct((STEPS, LANES), jnp...]
where the time goes in v7:
time: 61.1 us; the launch traced here: 60.1 us
  Pallas kernels  59.5 us (97%)
    pallas_call x1, Pallas kernels, shards(): pl.pallas_call(kernel, out_shape=jax.ShapeDtypeStruct((STEPS, LANES), jnp...  59.5 us

profile of v7, /device:TPU:1, one launch (start us, length us, event | category | flops | bytes accessed | tf_op | source)
XLA Modules:
  0.0 60.1 jit_solution(13900668922709755083)
XLA Ops:
  0.0 59.5 %match.1 = f32[8,128]{1,0:T(8,128)S(1)} custom-call(bf16[1024,1024]{1,0:T(8,128)(2,1)} %emb.1, s32[257]{0:T(512)} %offs.1), custom_call_target="tpu_custom_call" | custom-call | tf_op jit(solution)/shard_map/match/pallas_call | solution.py:426
  59.5 0.6 copy.4

commit v8 on v7

--- a/solution.py
+++ b/solution.py
@@ -46,6 +46,7 @@
     partner = device(0, 1 - core)
 
     last = x == 3
+    distant = ((work // 8) == 3) & ((x == 1) | (x == 2))
     to_base = jnp.where(last, -4, 0)
     to_near = to_base + 1
     to_far = to_base + 3
@@ -326,6 +327,18 @@
         )
 
     def advance(step, _):
+        near_copy(step).wait_recv()
+        swap_copy(step).start()
+
+        @pl.when(distant)
+        def _():
+            swap_copy(step).wait_recv()
+            scores = dot(own[...], gathered[step, NEAR * CHUNK:EXTRA * CHUNK, :])
+            row_base[...] = fold(
+                scores, id_own[...], [lanes_of(step, kind) for kind in (NEAR, SWAP)],
+                row_base[...], [(step, kind) for kind in (NEAR, SWAP)],
+            )
+
         @pl.when(has_far)
         def _():
             far_copy(step).wait_recv()
@@ -336,15 +349,25 @@
             base_copy(step).wait_recv()
             pl.when(core == 1)(lambda: extra_base(step).start())
 
-        near_copy(step).wait_recv()
-        swap_copy(step).start()
         for known in range(1, STEPS):
             pl.when((step == known) & (x < 3))(functools.partial(older, known))
             pl.when((step == known) & last)(functools.partial(older_both, known))
         pl.when(has_extra)(lambda: extra_own(step).wait_recv())
-        swap_copy(step).wait_recv()
-
-        @pl.when(x < 3)
+        pl.when(jnp.logical_not(distant))(lambda: swap_copy(step).wait_recv())
+
+        @pl.when(distant)
+        def _():
+            right = jnp.concatenate(
+                [gathered[step, FAR * CHUNK:NEAR * CHUNK, :], gathered[step, EXTRA * CHUNK:, :]],
+                axis=0,
+            )
+            row_base[...] = fold(
+                dot(own[...], right), id_own[...],
+                [lanes_of(step, kind) for kind in (FAR, EXTRA)],
+                row_base[...], [(step, kind) for kind in (FAR, EXTRA)],
+            )
+
+        @pl.when((x < 3) & jnp.logical_not(distant))
         def _():
             scores = dot(own[...], gathered[step, FAR * CHUNK:, :])
             row_base[...] = fold(

time: 61.1 us -> 61.2 us (level)
  no operation moved by 1% of the time
where the time goes in v8:
time: 61.2 us; the launch traced here: 60.1 us
  Pallas kernels  59.5 us (97%)
    pallas_call x1, Pallas kernels, shards(): pl.pallas_call(kernel, out_shape=jax.ShapeDtypeStruct((STEPS, LANES), jnp...  59.5 us

profile of v8, /device:TPU:1, one launch (start us, length us, event | category | flops | bytes accessed | tf_op | source)
XLA Modules:
  0.0 60.1 jit_solution(16024403389123939689)
XLA Ops:
  0.0 59.5 %match.1 = f32[8,128]{1,0:T(8,128)S(1)} custom-call(bf16[1024,1024]{1,0:T(8,128)(2,1)} %emb.1, s32[257]{0:T(512)} %offs.1), custom_call_target="tpu_custom_call" | custom-call | tf_op jit(solution)/shard_map/match/pallas_call | solution.py:449
  59.5 0.6 copy.4
